TPU v7x, 1024 devices: a whole 8x8x8 slice. The times are simulated.
1024 devices in a mesh: section: 4 (over y_lo), expert: 64 (over z, x), dp: 4 (over y_hi, core).
Axes of the slice: x: 8, y: 8 (y_hi: 2, y_lo: 4; y = y_hi * 4 + y_lo), z: 8, core: 2. Of those that a mesh axis runs over, the one named last changes fastest.
Arguments:
- upstream: bfloat16 [32768, 2048], P(('expert', 'dp')), may hold values from -6 to 6
- expert_ids: int32 [32768, 2], P(('expert', 'dp')), may hold values from 0 to 255, all different within a row; in each aligned block of 128 rows (0 to 127, 128 to 255, ...) at most 2 rows name the same one
- gate_index: int32 [32768, 2], P(('expert', 'dp')), may hold values from 0 to 63
- gate_table: float32 [64], replicated, may hold values from 0.1 to 1
- w_up: bfloat16 [256, 2048, 1408], P(('expert', 'dp'), 'section'), may hold values from -0.125 to 0.125
- w_down: bfloat16 [256, 1408, 2048], P(('expert', 'dp'), 'section'), may hold values from -0.15625 to 0.15625
- saved_pre: bfloat16 [256, 256, 2, 1408], P(('expert', 'dp'), None, None, 'section'), may hold values from -6 to 6
Outputs:
- grad_input: bfloat16 [32768, 2048], P(('expert', 'dp'), 'section')
Inputs may be any that keep to these rules, and one draw needn't show every extreme that they name: `expert_ids`: A token's 2 experts are different; within each aligned block of 128 tokens no expert is named more than 2 times, a bound that some block reaches.
All inputs are finite; a program needn't handle non-finite values.
Results may differ from a plain program's by a relative error of at most 0.0044.
Values may be sent and summed in bfloat16 or wider, within the bound.
No kernel may reach another device: no remote copies, remote signals or barrier semaphores. Data moves between devices by JAX's collectives and lax.ppermute only.
A program may use at most 32 MiB of HBM per device.

v0:
```python
import jax
import jax.numpy as jnp
from jax import lax
from jax.sharding import PartitionSpec as P


def body(upstream, expert_ids, gate_index, gate_table, w_up, w_down, saved_pre):
    model_width = upstream.shape[1]
    section_count = lax.axis_size("section")
    col_part = model_width // section_count
    section_here = lax.axis_index("section")
    groups = lax.axis_size("expert")
    members = lax.axis_size("dp")
    experts = groups * members
    capacity = saved_pre.shape[2]
    levels = gate_table.shape[0]
    hidden_part = w_down.shape[1]
    slot_count = experts * capacity
    chosen = (expert_ids[:, :, None] == jnp.arange(experts, dtype=jnp.int32)).astype(jnp.int32)
    per_token = jnp.sum(chosen, axis=1)
    earlier = jnp.cumsum(per_token, axis=0) - per_token
    places = expert_ids * capacity + jnp.sum(chosen * earlier[:, None, :], axis=2)
    gate_values = jnp.sum(
        jnp.where(gate_index[:, :, None] == jnp.arange(levels, dtype=jnp.int32), gate_table, 0.0),
        axis=2,
    )
    own_cols = lax.dynamic_slice_in_dim(upstream, section_here * col_part, col_part, 1)
    width_now = upstream.shape[1]
    sent_rows = (gate_values[:, :, None] * upstream.astype(jnp.float32)[:, None, :]).astype(
        jnp.bfloat16
    )
    filled = (
        jnp.zeros((slot_count, width_now), jnp.bfloat16)
        .at[places.reshape(-1)]
        .set(sent_rows.reshape(-1, width_now))
    )
    arrived = lax.all_to_all(
        lax.all_to_all(
            filled.reshape(groups, members, capacity, width_now),
            "expert",
            split_axis=0,
            concat_axis=0,
            tiled=True,
        ),
        "dp",
        split_axis=1,
        concat_axis=1,
        tiled=True,
    )
    proj_grad = jnp.einsum(
        "sd,fd->sf",
        arrived.reshape(slot_count, model_width),
        w_down[0],
        preferred_element_type=jnp.float32,
    )
    pre_act = saved_pre[0].reshape(slot_count, hidden_part).astype(jnp.float32)
    sig_value = jax.nn.sigmoid(pre_act)
    hid_grad = (proj_grad * (sig_value * (1.0 + pre_act * (1.0 - sig_value)))).astype(jnp.bfloat16)
    weights = w_up[0]
    back_rows = jnp.einsum(
        "sf,df->sd",
        lax.all_gather(hid_grad, "section", axis=1, tiled=True),
        weights,
        preferred_element_type=jnp.float32,
    )
    back_rows = back_rows.astype(jnp.bfloat16).reshape(groups, members, capacity, col_part)
    returned = lax.all_to_all(
        lax.all_to_all(back_rows, "expert", split_axis=0, concat_axis=0, tiled=True),
        "dp",
        split_axis=1,
        concat_axis=1,
        tiled=True,
    )
    flat_rows = returned.reshape(slot_count, col_part)
    picked = flat_rows[places]
    result = own_cols.astype(jnp.float32) + jnp.sum(picked.astype(jnp.float32), axis=1)
    return result.astype(jnp.bfloat16)


def solution(mesh):
    in_specs = (
        P(("expert", "dp"), None),
        P(("expert", "dp"), None),
        P(("expert", "dp"), None),
        P(),
        P(("expert", "dp"), "section", None),
        P(("expert", "dp"), "section", None),
        P(("expert", "dp"), None, None, "section"),
    )
    out_specs = P(("expert", "dp"), "section")
    return jax.shard_map(body, mesh=mesh, in_specs=in_specs, out_specs=out_specs, check_vma=False)
```

profile of v0, /device:TPU:1, one launch (start us, length us, event | category | flops | bytes accessed | tf_op | source)
XLA Modules:
  0.0 278.9 jit_solution(10249593157913297388)
XLA Ops:
  6.5 0.9 convert_reduce_fusion
  9.5 3.4 %mul.51 = f32[128,2,2048]{2,1,0:T(2,128)} broadcast(bf16[128,2048]{1,0:T(8,128)(2,1)} %param.7), dimensions={0,2} | broadcast | bytes 2621440 | tf_op jit(solution)/shard_map/mul | solution.py:29
  12.9 2.7 mul.52
  17.1 1.0 mul.49
  18.1 3.8 %scatter_custom_fusion = bf16[512,2048]{1,0:T(8,128)(2,1)} fusion(s32[256]{0:T(256)S(1)} %bitcast.15, f32[256,2048]{1,0:T(8,128)S(1)} %mul.52, f32[256]{0:T(256)S(1)} %mul.49, bf16[]{:T(256)} %constant.5.clone.1), kind=kCustom, calls=%fused_computation.10 | custom fusion | flops 1048576 | bytes 4195330 | tf_op jit(solution)/shard_map/scatter | solution.py:35
  21.9 3.2 %reshape.63 = bf16[64,4,2,2048]{3,2,1,0:T(2,128)(2,1)S(1)} reshape(bf16[512,2048]{1,0:T(8,128)(2,1)} %scatter_custom_fusion) | data formatting | bytes 4194304 | tf_op jit(solution)/shard_map/reshape | solution.py:39
  25.1 72.3 %all_to_all.20 = bf16[64,4,2,2048]{3,2,1,0:T(2,128)(2,1)S(1)} all-to-all(bf16[64,4,2,2048]{3,2,1,0:T(2,128)(2,1)S(1)} %reshape.63), channel_id=1, replica_groups=mesh['section'=4,'expert'=64,'dp'=4] {'expert'}, dimensions={0} | all-to-all | bytes 4194304 | tf_op jit(solution)/shard_map/all_to_all | solution.py:38
  97.4 3.0 %copy.48 = bf16[64,4,2,2048]{3,2,0,1:T(2,128)(2,1)} copy(bf16[64,4,2,2048]{3,2,1,0:T(2,128)(2,1)S(1)} %all_to_all.20) | data formatting | bytes 4194304 | tf_op jit(solution)/shard_map/all_to_all | solution.py:38
  100.4 11.6 %all-to-all-start.1 = ((bf16[64,4,2,2048]{3,2,0,1:T(2,128)(2,1)}), bf16[64,4,2,2048]{3,2,0,1:T(2,128)(2,1)S(1)}, u32[]{:S(2)}, u32[]{:S(2)}) async-start(bf16[64,4,2,2048]{3,2,0,1:T(2,128)(2,1)} %copy.48), calls=%async_computation.1 | async-start | bytes 4194304 | tf_op jit(solution)/shard_map/all_to_all | solution.py:37
  111.9 2.0 copy.50
  113.9 2.6 reshape.67
  116.5 2.3 copy.51
  118.7 32.4 %all-to-all-done.1 = bf16[64,4,2,2048]{3,2,0,1:T(2,128)(2,1)S(1)} async-done(((bf16[64,4,2,2048]{3,2,0,1:T(2,128)(2,1)}), bf16[64,4,2,2048]{3,2,0,1:T(2,128)(2,1)S(1)}, u32[]{:S(2)}, u32[]{:S(2)}) %all-to-all-start.1) | async-done | bytes 2097184 | tf_op jit(solution)/shard_map/all_to_all | solution.py:37
  151.1 3.8 %copy.49 = bf16[64,4,2,2048]{3,2,1,0:T(2,128)(2,1)} copy(bf16[64,4,2,2048]{3,2,0,1:T(2,128)(2,1)S(1)} %all-to-all-done.1) | data formatting | bytes 4194304 | tf_op jit(solution)/shard_map/all_to_all | solution.py:37
  154.9 2.7 reshape.64
  157.7 3.3 %fusion.10 = bf16[512,352]{0,1:T(8,128)(2,1)} fusion(bf16[512,2048]{1,0:T(8,128)(2,1)S(1)} %reshape.64, bf16[1,352,2048]{2,1,0:T(8,128)(2,1)} %param.12, f32[512,352]{0,1:T(8,128)} %copy.51), kind=kOutput, calls=%fused_computation.9 | convolution fusion | flops 739819520 | bytes 4620288 | tf_op jit(solution)/shard_map/sd,fd->sf/dot_general | solution.py:50
  161.0 49.5 %all-gather.2.cloned.1.call-done = bf16[512,1408]{0,1:T(8,128)(2,1)} async-done(((bf16[512,352]{0,1:T(8,128)(2,1)}), bf16[512,1408]{0,1:T(8,128)(2,1)}) %all-gather.2.cloned.1.call-update) | async-done | bytes 1441808 | tf_op jit(solution)/shard_map/all_gather | solution.py:62
  210.6 2.4 fusion.4
  213.2 30.3 %all_to_all.21 = bf16[64,4,2,512]{3,2,1,0:T(2,128)(2,1)S(1)} all-to-all(bf16[64,4,2,512]{3,2,1,0:T(2,128)(2,1)S(1)} %reshape.65), channel_id=1, replica_groups=mesh['section'=4,'expert'=64,'dp'=4] {'expert'}, dimensions={0} | all-to-all | bytes 1048576 | tf_op jit(solution)/shard_map/all_to_all | solution.py:68
  243.5 1.1 copy.53
  244.6 9.1 %all-to-all-start.3 = ((bf16[64,4,2,512]{3,2,0,1:T(2,128)(2,1)}), bf16[64,4,2,512]{3,2,0,1:T(2,128)(2,1)S(1)}, u32[]{:S(2)}, u32[]{:S(2)}) async-start(bf16[64,4,2,512]{3,2,0,1:T(2,128)(2,1)} %copy.53), calls=%async_computation.3 | async-start | bytes 1048576 | tf_op jit(solution)/shard_map/all_to_all | solution.py:67
  254.0 13.8 %all-to-all-done.3 = bf16[64,4,2,512]{3,2,0,1:T(2,128)(2,1)S(1)} async-done(((bf16[64,4,2,512]{3,2,0,1:T(2,128)(2,1)}), bf16[64,4,2,512]{3,2,0,1:T(2,128)(2,1)S(1)}, u32[]{:S(2)}, u32[]{:S(2)}) %all-to-all-start.3) | async-done | bytes 524320 | tf_op jit(solution)/shard_map/all_to_all | solution.py:67
  268.4 1.2 gather_fusion
  270.5 1.6 add_convert_fusion
  (23 shorter events, 5.5 us)
Async XLA Ops:
  6.5 204.0 %copy-start = (bf16[1,512,1408]{2,1,0:T(8,128)(2,1)S(1)}, bf16[1,512,1408]{2,1,0:T(8,128)(2,1)}, u32[]{:S(2)}) copy-start(bf16[1,512,1408]{2,1,0:T(8,128)(2,1)} %param.11) | copy-start | bytes 4325380
  12.9 2.7 copy-start.1
  100.4 50.8 %all-to-all-start.1 = ((bf16[64,4,2,2048]{3,2,0,1:T(2,128)(2,1)}), bf16[64,4,2,2048]{3,2,0,1:T(2,128)(2,1)S(1)}, u32[]{:S(2)}, u32[]{:S(2)}) async-start(bf16[64,4,2,2048]{3,2,0,1:T(2,128)(2,1)} %copy.48), calls=%async_computation.1 | async-start | bytes 4194304 | tf_op jit(solution)/shard_map/all_to_all | solution.py:37
  111.9 98.6 %all-gather.2.cloned.1.call-start = ((), (), s32[]{:S(2)}) async-start(), calls=%async_computation.4 | async-start | bytes 1802240 | tf_op jit(solution)/shard_map/all_gather | solution.py:62
  244.6 23.2 %all-to-all-start.3 = ((bf16[64,4,2,512]{3,2,0,1:T(2,128)(2,1)}), bf16[64,4,2,512]{3,2,0,1:T(2,128)(2,1)S(1)}, u32[]{:S(2)}, u32[]{:S(2)}) async-start(bf16[64,4,2,512]{3,2,0,1:T(2,128)(2,1)} %copy.53), calls=%async_computation.3 | async-start | bytes 1048576 | tf_op jit(solution)/shard_map/all_to_all | solution.py:67
Sparse Core Ops, SparseCore 0:
  161.2 49.3 all-gather.1
where the time goes:
time: 281 us; the launch traced here: 279 us
  blocking collectives  103 us (37%)
  waiting for transfers between devices  95.7 us (34%)
  local copies, waits for them, and re-layouts  31.3 us (11%)
  starting transfers between devices  20.7 us (7%)
  between operations  13.5 us (5%)
  other arithmetic  9.43 us (3%)
  matrix products  5.72 us (2%)
    all_to_all x1, blocking collectives, body(): lax.all_to_all(filled.reshape(groups, members, capacity, width_now), 'exp...  72.3 us
    all_gather x1, waiting for transfers between devices, body(): lax.all_gather(hid_grad, 'section', axis=1, tiled=True)  49.5 us
    all_to_all x1, waiting for transfers between devices, body(): lax.all_to_all(lax.all_to_all(filled.reshape(groups, members, capacity, w...  32.4 us
    all_to_all x1, blocking collectives, body(): lax.all_to_all(back_rows, 'expert', split_axis=0, concat_axis=0, tiled=True)  30.3 us
    all_to_all x1, waiting for transfers between devices, body(): lax.all_to_all(lax.all_to_all(back_rows, 'expert', split_axis=0, concat_a...  13.8 us
    all_to_all x1, starting transfers between devices, body(): lax.all_to_all(lax.all_to_all(filled.reshape(groups, members, capacity, w...  11.6 us
    all_to_all x1, starting transfers between devices, body(): lax.all_to_all(lax.all_to_all(back_rows, 'expert', split_axis=0, concat_a...  9.09 us
    mul x3, local copies, waits for them, and re-layouts, body(): gate_values[:, :, None] * upstream.astype(jnp.float32)[:, None, :]  7.13 us
  transfers between devices with their start and end apart: 3, of which 3 were waited for; matrix products, arithmetic and copies ran while one was open for 3% of the time, Pallas kernels for 0%

commit v1 on v0

v1 whole, which is shorter than its diff:
```python
import jax
import jax.numpy as jnp
from jax import lax
from jax.sharding import PartitionSpec as P

NEAR = [(0, 1), (1, 0), (2, 3), (3, 2)]
FAR = [(0, 2), (2, 0), (1, 3), (3, 1)]
CROSS = [((3, 0), (0, 1)), ((0, 1), (3, 0)), ((0, 0), (2, 1)), ((3, 1), (1, 0))]


def cross_pairs():
    pairs = []
    for (s0, h0), (s1, h1) in CROSS:
        for core in range(2):
            pairs.append((s0 * 4 + h0 * 2 + core, s1 * 4 + h1 * 2 + core))
    return pairs


def ranks_of(flat_ids, tokens):
    pair = jnp.arange(flat_ids.shape[0], dtype=jnp.int32)
    token = jnp.where(pair >= tokens, pair - tokens, pair)
    same = (flat_ids[:, None] == flat_ids[None, :]) & (token[:, None] < token[None, :])
    return jnp.sum(same.astype(jnp.int32), axis=0)


def body(upstream, expert_ids, gate_index, gate_table, w_up, w_down, saved_pre):
    tokens, model_width = upstream.shape
    col_part = model_width // lax.axis_size("section")
    groups = lax.axis_size("expert")
    levels = gate_table.shape[0]
    capacity = saved_pre.shape[2]
    hidden_part = w_down.shape[1]
    section = lax.axis_index("section")
    member = lax.axis_index("dp")
    half = member // 2
    kind = section % 2
    hidden_pair = section // 2
    slots = groups * 2 * capacity

    weight_own = w_down[0]
    weight_other = lax.ppermute(weight_own, "section", NEAR)
    pre = saved_pre[0].reshape(groups, 2, 2, capacity, hidden_part)
    pre_mine = jnp.where(kind == 0, pre[:, 0], pre[:, 1]).reshape(slots, hidden_part)
    pre_theirs = jnp.where(kind == 0, pre[:, 1], pre[:, 0]).reshape(slots, hidden_part)
    pre_mine = pre_mine.T
    pre_other = lax.ppermute(pre_theirs.T, "section", NEAR)

    packed = expert_ids.T * levels + gate_index.T
    crossing = kind != half
    packed_in = lax.ppermute(packed, ("section", "dp"), cross_pairs())
    block_in = lax.ppermute(upstream, ("section", "dp"), cross_pairs())
    served = jnp.where(crossing, packed_in, packed).reshape(-1)
    block = jnp.where(crossing, block_in, upstream)

    ids = served // levels
    gates = jnp.sum(
        jnp.where(
            (served % levels)[None, :] == jnp.arange(levels, dtype=jnp.int32)[:, None],
            gate_table[:, None],
            0.0,
        ),
        axis=0,
    )
    here = (ids % 4) // 2 == half
    row = jnp.where(here, ((ids // 4) * 2 + ids % 2) * capacity + ranks_of(ids, tokens), -1)
    match = row[None, :] == jnp.arange(slots, dtype=jnp.int32)[:, None]
    row_gate = jnp.sum(jnp.where(match, gates[None, :], 0.0), axis=1)
    chosen = (match[:, :tokens] | match[:, tokens:]).astype(jnp.bfloat16)
    picked = jnp.dot(chosen, block, preferred_element_type=jnp.float32)
    rows = (row_gate[:, None] * picked).astype(jnp.bfloat16)
    halves = [[g * 4 + h * 2 + c for g in range(groups) for c in range(2)] for h in range(2)]
    arrived = lax.all_to_all(
        rows.reshape(groups * 2, capacity, model_width),
        ("expert", "dp"),
        split_axis=0,
        concat_axis=0,
        axis_index_groups=halves,
        tiled=True,
    ).reshape(slots, model_width)

    def hidden_grad(weight, pre_act):
        proj = jnp.einsum("fd,sd->fs", weight, arrived, preferred_element_type=jnp.float32)
        pre_act = pre_act.astype(jnp.float32)
        sig = jax.nn.sigmoid(pre_act)
        return (proj * (sig * (1.0 + pre_act * (1.0 - sig)))).astype(jnp.bfloat16)

    hid_own = hidden_grad(weight_own, pre_mine)
    hid_other = hidden_grad(weight_other, pre_other)
    hid = jnp.concatenate(
        [jnp.where(kind == 0, hid_own, hid_other), jnp.where(kind == 0, hid_other, hid_own)]
    )
    far = lax.ppermute(hid, "section", FAR)
    near = lax.ppermute(hid, "section", NEAR)
    far_near = lax.ppermute(far, "section", NEAR)

    def back(own_pair, other_pair):
        whole = jnp.concatenate(
            [
                jnp.where(hidden_pair == 0, own_pair, other_pair),
                jnp.where(hidden_pair == 0, other_pair, own_pair),
            ]
        )
        out = jnp.einsum("fs,df->sd", whole, w_up[0], preferred_element_type=jnp.float32)
        return out.astype(jnp.bfloat16).reshape(groups, 2, capacity, col_part)

    mine, theirs = back(hid, far), back(near, far_near)
    back_rows = jnp.stack(
        [jnp.where(kind == 0, mine, theirs), jnp.where(kind == 0, theirs, mine)], axis=1
    ).reshape(groups * 4, capacity, col_part)
    returned = lax.all_to_all(
        back_rows, ("expert", "dp"), split_axis=0, concat_axis=0, tiled=True
    ).reshape(groups * 4 * capacity, col_part)

    flat_ids = expert_ids.T.reshape(-1)
    places = flat_ids * capacity + ranks_of(flat_ids, tokens)
    wanted = places[:, None] == jnp.arange(groups * 4 * capacity, dtype=jnp.int32)
    wanted = (wanted[:tokens] | wanted[tokens:]).astype(jnp.bfloat16)
    total = jnp.dot(wanted, returned, preferred_element_type=jnp.float32)
    own_cols = lax.dynamic_slice_in_dim(upstream, section * col_part, col_part, 1)
    return (own_cols.astype(jnp.float32) + total).astype(jnp.bfloat16)


def solution(mesh):
    in_specs = (
        P(("expert", "dp"), None),
        P(("expert", "dp"), None),
        P(("expert", "dp"), None),
        P(),
        P(("expert", "dp"), "section", None),
        P(("expert", "dp"), "section", None),
        P(("expert", "dp"), None, None, "section"),
    )
    out_specs = P(("expert", "dp"), "section")
    return jax.shard_map(body, mesh=mesh, in_specs=in_specs, out_specs=out_specs, check_vma=False)
```

time: 281 us -> 172 us (0.61)
  blocking collectives: 103 us -> 0 us
  starting transfers between devices: 20.7 us -> 76.2 us
  local copies, waits for them, and re-layouts: 31.3 us -> 4.97 us
  waiting for transfers between devices: 95.7 us -> 76.1 us
  between operations: 13.5 us -> 0.33 us
  other arithmetic: 9.43 us -> 4.8 us
  matrix products: 5.72 us -> 8.58 us
    all_to_all x2 -> x0, blocking collectives: 103 us -> none  [the longest x1 72.3 us: body(): lax.all_to_all(filled.reshape(groups, members, capacity, width_now), 'exp...]
    all_gather x1 -> x0, waiting for transfers between devices: 49.5 us -> none  [body(): lax.all_gather(hid_grad, 'section', axis=1, tiled=True)]
    all_to_all x2, starting transfers between devices: 20.7 us -> 50.4 us  [the longest x1 29 us: body(): lax.all_to_all(rows.reshape(groups * 2, capacity, model_width), ('expert'...]
    ppermute x0 -> x7, waiting for transfers between devices: none -> 28.5 us  [the longest x1 12.6 us: body(): far = lax.ppermute(hid, 'section', FAR)]
    ppermute x0 -> x7, starting transfers between devices: none -> 25.8 us  [the longest x1 7.38 us: body(): packed_in = lax.ppermute(packed, ('section', 'dp'), cross_pairs())]
    all_to_all x4 -> x0, local copies, waits for them, and re-layouts: 8.31 us -> none  [the longest x1 3.82 us: body(): lax.all_to_all(lax.all_to_all(filled.reshape(groups, members, capacity, w...]
    mul x3 -> x0, local copies, waits for them, and re-layouts: 7.13 us -> none  [body(): gate_values[:, :, None] * upstream.astype(jnp.float32)[:, None, :]]
    convert_element_type x4 -> x2, local copies, waits for them, and re-layouts: 7.14 us -> 1.17 us  [hidden_grad(): pre_act = pre_act.astype(jnp.float32)]
  transfers between devices with their start and end apart: 3 -> 9, of which waited for: 3 -> 6; matrix products, arithmetic and copies ran while one was open for 3% -> 5% of each run, Pallas kernels for 0% -> 0%
where the time goes in v1:
time: 172 us; the launch traced here: 171 us
  starting transfers between devices  76.2 us (44%)
  waiting for transfers between devices  76.1 us (44%)
  matrix products  8.58 us (5%)
  local copies, waits for them, and re-layouts  4.97 us (3%)
  other arithmetic  4.8 us (3%)
    all_to_all x1, starting transfers between devices, body(): lax.all_to_all(rows.reshape(groups * 2, capacity, model_width), ('expert'...  29 us
    all_to_all x1, waiting for transfers between devices, body(): lax.all_to_all(back_rows, ('expert', 'dp'), split_axis=0, concat_axis=0,...  25 us
    all_to_all x1, waiting for transfers between devices, body(): lax.all_to_all(rows.reshape(groups * 2, capacity, model_width), ('expert'...  22.7 us
    all_to_all x1, starting transfers between devices, body(): lax.all_to_all(back_rows, ('expert', 'dp'), split_axis=0, concat_axis=0,...  21.4 us
    ppermute x1, waiting for transfers between devices, body(): far = lax.ppermute(hid, 'section', FAR)  12.6 us
    ppermute x1, starting transfers between devices, body(): packed_in = lax.ppermute(packed, ('section', 'dp'), cross_pairs())  7.38 us
    ppermute x1, waiting for transfers between devices, body(): far_near = lax.ppermute(far, 'section', NEAR)  6.41 us
    ppermute x1, starting transfers between devices, body(): far = lax.ppermute(hid, 'section', FAR)  5.66 us
  transfers between devices with their start and end apart: 9, of which 6 were waited for; matrix products, arithmetic and copies ran while one was open for 5% of the time, Pallas kernels for 0%

profile of v1, /device:TPU:1, one launch (start us, length us, event | category | flops | bytes accessed | tf_op | source)
XLA Modules:
  0.0 171.1 jit_solution(2804552262914304302)
XLA Ops:
  0.8 7.4 %collective-permute-start = (s32[2,128]{1,0:T(2,128)S(1)}, s32[2,128]{1,0:T(2,128)S(1)}, u32[]{:S(2)}, u32[]{:S(2)}) collective-permute-start(s32[2,128]{1,0:T(2,128)S(1)} %bitcast_add_fusion), channel_id=1, source_target_pairs={{768,2},{769,3},{2,768},{3,769},{0,514},{1,515},{770,256},{771,257... | collective-permute-start | bytes 3080 | tf_op jit(solution)/shard_map/ppermute | solution.py:50
  8.2 1.3 collective-permute-start.1
  10.4 0.9 convert_reduce_fusion.1
  11.5 4.5 %collective-permute-done.1 = bf16[128,2048]{1,0:T(8,128)(2,1)S(1)} collective-permute-done((bf16[128,2048]{1,0:T(8,128)(2,1)}, bf16[128,2048]{1,0:T(8,128)(2,1)S(1)}, u32[]{:S(2)}, u32[]{:S(2)}) %collective-permute-start.1) | collective-permute-done | bytes 524320 | tf_op jit(solution)/shard_map/ppermute | solution.py:51
  16.0 1.5 fusion
  17.5 1.5 reshape.247
  19.0 29.0 %all-to-all-start = ((bf16[128,2,2048]{2,1,0:T(2,128)(2,1)}), bf16[128,2,2048]{2,1,0:T(2,128)(2,1)S(1)}, u32[]{:S(2)}, u32[]{:S(2)}) async-start(bf16[128,2,2048]{2,1,0:T(2,128)(2,1)} %reshape.247), calls=%async_computation | async-start | bytes 2097152 | tf_op jit(solution)/shard_map/all_to_all | solution.py:72
  48.0 1.9 %collective-permute-start.2 = (bf16[352,2048]{1,0:T(8,128)(2,1)}, bf16[352,2048]{1,0:T(8,128)(2,1)}, u32[]{:S(2)}, u32[]{:S(2)}) collective-permute-start(bf16[352,2048]{1,0:T(8,128)(2,1)} %bitcast.85), channel_id=1, source_target_pairs={{0,256},{256,0},{512,768},{768,512},{1,257},{257,1},{513,769},{769... | collective-permute-start | bytes 4325384 | tf_op jit(solution)/shard_map/ppermute | solution.py:41
  50.9 0.8 copy.17
  51.7 3.4 %collective-permute-start.3 = (bf16[352,256]{1,0:T(8,128)(2,1)}, bf16[352,256]{1,0:T(8,128)(2,1)}, u32[]{:S(2)}, u32[]{:S(2)}) collective-permute-start(bf16[352,256]{1,0:T(8,128)(2,1)} %bitcast.10), channel_id=1, source_target_pairs={{0,256},{256,0},{512,768},{768,512},{1,257},{257,1},{513,769},{769... | collective-permute-start | bytes 540680 | tf_op jit(solution)/shard_map/ppermute | solution.py:46
  55.4 0.9 copy.16
  56.3 22.7 %all-to-all-done = bf16[128,2,2048]{2,1,0:T(2,128)(2,1)S(1)} async-done(((bf16[128,2,2048]{2,1,0:T(2,128)(2,1)}), bf16[128,2,2048]{2,1,0:T(2,128)(2,1)S(1)}, u32[]{:S(2)}, u32[]{:S(2)}) %all-to-all-start) | async-done | bytes 1048608 | tf_op jit(solution)/shard_map/all_to_all | solution.py:72
  79.3 2.0 %fusion.13 = bf16[352,256]{1,0:T(8,128)(2,1)S(1)} fusion(bf16[256,2048]{1,0:T(8,128)(2,1)S(1)} %reshape.248, f32[256,352]{0,1:T(8,128)} %copy.16, bf16[1,352,2048]{2,1,0:T(8,128)(2,1)} %param.12), kind=kOutput, calls=%fused_computation.12 | convolution fusion | flops 369909760 | bytes 3031040 | tf_op jit(solution)/shard_map/fd,sd->fs/dot_general | solution.py:82
  81.3 4.9 %collective-permute-done.3 = bf16[352,256]{1,0:T(8,128)(2,1)} collective-permute-done((bf16[352,256]{1,0:T(8,128)(2,1)}, bf16[352,256]{1,0:T(8,128)(2,1)}, u32[]{:S(2)}, u32[]{:S(2)}) %collective-permute-start.3) | collective-permute-done | bytes 180256 | tf_op jit(solution)/shard_map/ppermute | solution.py:46
  86.3 2.0 %broadcast_select_fusion.9 = (bf16[352,256]{1,0:T(8,128)(2,1)S(1)}, bf16[352,256]{1,0:T(8,128)(2,1)S(1)}) fusion(bf16[352,256]{1,0:T(8,128)(2,1)S(1)} %fusion.13, pred[]{:T(512)S(6)} %eq.101, bf16[352,256]{1,0:T(8,128)(2,1)} %collective-permute-done.3, bf16[256,2048]{1,0:T(8,128)(2,1)S(1)} %reshape.248, bf16[352,2048]{1,0:T(8,128)(2,1)} %collective-permute-done.2), kind=kOutput, calls=%fused_computation.59 | convolution fusion | flops 370180096 | bytes 3211265 | tf_op jit(solution)/shard_map/fd,sd->fs/dot_general | solution.py:82
  88.3 5.7 %collective-permute-start.4 = (bf16[704,256]{1,0:T(8,128)(2,1)S(1)}, bf16[704,256]{1,0:T(8,128)(2,1)S(1)}, u32[]{:S(2)}, u32[]{:S(2)}) collective-permute-start(bf16[704,256]{1,0:T(8,128)(2,1)S(1)} %pad_maximum_fusion.1), channel_id=1, source_target_pairs={{0,512},{512,0},{256,768},{768,256},{1,513},{513,1},{257,769},{769... | collective-permute-start | bytes 1081352 | tf_op jit(solution)/shard_map/ppermute | solution.py:92
  94.0 3.0 %collective-permute-start.5 = (bf16[704,256]{1,0:T(8,128)(2,1)S(1)}, bf16[704,256]{1,0:T(8,128)(2,1)S(1)}, u32[]{:S(2)}, u32[]{:S(2)}) collective-permute-start(bf16[704,256]{1,0:T(8,128)(2,1)S(1)} %pad_maximum_fusion.1), channel_id=1, source_target_pairs={{0,256},{256,0},{512,768},{768,512},{1,257},{257,1},{513,769},{769... | collective-permute-start | bytes 1081352 | tf_op jit(solution)/shard_map/ppermute | solution.py:93
  97.0 12.6 %collective-permute-done.4 = bf16[704,256]{1,0:T(8,128)(2,1)S(1)} collective-permute-done((bf16[704,256]{1,0:T(8,128)(2,1)S(1)}, bf16[704,256]{1,0:T(8,128)(2,1)S(1)}, u32[]{:S(2)}, u32[]{:S(2)}) %collective-permute-start.4) | collective-permute-done | bytes 360480 | tf_op jit(solution)/shard_map/ppermute | solution.py:92
  109.7 3.2 %collective-permute-start.6 = (bf16[704,256]{1,0:T(8,128)(2,1)S(1)}, bf16[704,256]{1,0:T(8,128)(2,1)S(1)}, u32[]{:S(2)}, u32[]{:S(2)}) collective-permute-start(bf16[704,256]{1,0:T(8,128)(2,1)S(1)} %collective-permute-done.4), channel_id=1, source_target_pairs={{0,256},{256,0},{512,768},{768,512},{1,257},{257,1},{513,769},{769... | collective-permute-start | bytes 1081352 | tf_op jit(solution)/shard_map/ppermute | solution.py:94
  113.6 6.4 %collective-permute-done.6 = bf16[704,256]{1,0:T(8,128)(2,1)S(1)} collective-permute-done((bf16[704,256]{1,0:T(8,128)(2,1)S(1)}, bf16[704,256]{1,0:T(8,128)(2,1)S(1)}, u32[]{:S(2)}, u32[]{:S(2)}) %collective-permute-start.6) | collective-permute-done | bytes 360480 | tf_op jit(solution)/shard_map/ppermute | solution.py:94
  121.0 1.5 pad_maximum_fusion
  122.5 21.4 %all-to-all-start.1 = ((bf16[256,2,512]{2,1,0:T(2,128)(2,1)}), bf16[256,2,512]{2,1,0:T(2,128)(2,1)S(1)}, u32[]{:S(2)}, u32[]{:S(2)}) async-start(bf16[256,2,512]{2,1,0:T(2,128)(2,1)} %bitcast.14), calls=%async_computation.1 | async-start | bytes 1048576 | tf_op jit(solution)/shard_map/all_to_all | solution.py:110
  144.0 25.0 %all-to-all-done.1 = bf16[256,2,512]{2,1,0:T(2,128)(2,1)S(1)} async-done(((bf16[256,2,512]{2,1,0:T(2,128)(2,1)}), bf16[256,2,512]{2,1,0:T(2,128)(2,1)S(1)}, u32[]{:S(2)}, u32[]{:S(2)}) %all-to-all-start.1) | async-done | bytes 524320 | tf_op jit(solution)/shard_map/all_to_all | solution.py:110
  169.2 1.9 %fusion.15 = bf16[128,512]{1,0:T(8,128)(2,1)} fusion(bf16[512,512]{1,0:T(8,128)(2,1)S(1)} %reshape.250, pred[256,512]{1,0:T(32,128)(4,1)S(1)} %iota_compare_fusion, bf16[128,2048]{1,0:T(8,128)(2,1)} %param.7, s32[]{:T(128)S(6)} %select_n.201), kind=kOutput, calls=%fused_computation.15 | convolution fusion | flops 67371008 | bytes 917508 | tf_op jit(solution)/shard_map/dot_general | solution.py:118
  (31 shorter events, 5.4 us)
Async XLA Ops:
  0.0 113.0 %copy-start = (bf16[1,512,1408]{2,1,0:T(8,128)(2,1)S(1)}, bf16[1,512,1408]{2,1,0:T(8,128)(2,1)}, u32[]{:S(2)}) copy-start(bf16[1,512,1408]{2,1,0:T(8,128)(2,1)} %param.11) | copy-start | bytes 4325380
  0.8 8.8 %collective-permute-start = (s32[2,128]{1,0:T(2,128)S(1)}, s32[2,128]{1,0:T(2,128)S(1)}, u32[]{:S(2)}, u32[]{:S(2)}) collective-permute-start(s32[2,128]{1,0:T(2,128)S(1)} %bitcast_add_fusion), channel_id=1, source_target_pairs={{768,2},{769,3},{2,768},{3,769},{0,514},{1,515},{770,256},{771,257... | collective-permute-start | bytes 3080 | tf_op jit(solution)/shard_map/ppermute | solution.py:50
  8.2 7.8 %collective-permute-start.1 = (bf16[128,2048]{1,0:T(8,128)(2,1)}, bf16[128,2048]{1,0:T(8,128)(2,1)S(1)}, u32[]{:S(2)}, u32[]{:S(2)}) collective-permute-start(bf16[128,2048]{1,0:T(8,128)(2,1)} %param.7), channel_id=1, source_target_pairs={{768,2},{769,3},{2,768},{3,769},{0,514},{1,515},{770,256},{771,257... | collective-permute-start | bytes 1572872 | tf_op jit(solution)/shard_map/ppermute | solution.py:51
  19.0 31.0 %copy-start.1 = (bf16[1,256,2,352]{1,3,2,0:T(8,128)(2,1)S(1)}, bf16[1,256,2,352]{1,3,2,0:T(8,128)(2,1)}, u32[]{:S(2)}) copy-start(bf16[1,256,2,352]{1,3,2,0:T(8,128)(2,1)} %param.13) | copy-start | bytes 1081348
  19.0 59.9 %all-to-all-start = ((bf16[128,2,2048]{2,1,0:T(2,128)(2,1)}), bf16[128,2,2048]{2,1,0:T(2,128)(2,1)S(1)}, u32[]{:S(2)}, u32[]{:S(2)}) async-start(bf16[128,2,2048]{2,1,0:T(2,128)(2,1)} %reshape.247), calls=%async_computation | async-start | bytes 2097152 | tf_op jit(solution)/shard_map/all_to_all | solution.py:72
  48.0 38.3 %collective-permute-start.2 = (bf16[352,2048]{1,0:T(8,128)(2,1)}, bf16[352,2048]{1,0:T(8,128)(2,1)}, u32[]{:S(2)}, u32[]{:S(2)}) collective-permute-start(bf16[352,2048]{1,0:T(8,128)(2,1)} %bitcast.85), channel_id=1, source_target_pairs={{0,256},{256,0},{512,768},{768,512},{1,257},{257,1},{513,769},{769... | collective-permute-start | bytes 4325384 | tf_op jit(solution)/shard_map/ppermute | solution.py:41
  51.7 34.6 %collective-permute-start.3 = (bf16[352,256]{1,0:T(8,128)(2,1)}, bf16[352,256]{1,0:T(8,128)(2,1)}, u32[]{:S(2)}, u32[]{:S(2)}) collective-permute-start(bf16[352,256]{1,0:T(8,128)(2,1)} %bitcast.10), channel_id=1, source_target_pairs={{0,256},{256,0},{512,768},{768,512},{1,257},{257,1},{513,769},{769... | collective-permute-start | bytes 540680 | tf_op jit(solution)/shard_map/ppermute | solution.py:46
  88.3 21.4 %collective-permute-start.4 = (bf16[704,256]{1,0:T(8,128)(2,1)S(1)}, bf16[704,256]{1,0:T(8,128)(2,1)S(1)}, u32[]{:S(2)}, u32[]{:S(2)}) collective-permute-start(bf16[704,256]{1,0:T(8,128)(2,1)S(1)} %pad_maximum_fusion.1), channel_id=1, source_target_pairs={{0,512},{512,0},{256,768},{768,256},{1,513},{513,1},{257,769},{769... | collective-permute-start | bytes 1081352 | tf_op jit(solution)/shard_map/ppermute | solution.py:92
  94.0 19.6 %collective-permute-start.5 = (bf16[704,256]{1,0:T(8,128)(2,1)S(1)}, bf16[704,256]{1,0:T(8,128)(2,1)S(1)}, u32[]{:S(2)}, u32[]{:S(2)}) collective-permute-start(bf16[704,256]{1,0:T(8,128)(2,1)S(1)} %pad_maximum_fusion.1), channel_id=1, source_target_pairs={{0,256},{256,0},{512,768},{768,512},{1,257},{257,1},{513,769},{769... | collective-permute-start | bytes 1081352 | tf_op jit(solution)/shard_map/ppermute | solution.py:93
  109.7 10.4 %collective-permute-start.6 = (bf16[704,256]{1,0:T(8,128)(2,1)S(1)}, bf16[704,256]{1,0:T(8,128)(2,1)S(1)}, u32[]{:S(2)}, u32[]{:S(2)}) collective-permute-start(bf16[704,256]{1,0:T(8,128)(2,1)S(1)} %collective-permute-done.4), channel_id=1, source_target_pairs={{0,256},{256,0},{512,768},{768,512},{1,257},{257,1},{513,769},{769... | collective-permute-start | bytes 1081352 | tf_op jit(solution)/shard_map/ppermute | solution.py:94
  120.9 23.0 %copy-start.2 = (s32[128,2]{0,1:T(2,128)S(1)}, s32[128,2]{0,1:T(2,128)}, u32[]{:S(2)}) copy-start(s32[128,2]{0,1:T(2,128)} %param.8) | copy-start | bytes 3076
  122.5 46.5 %all-to-all-start.1 = ((bf16[256,2,512]{2,1,0:T(2,128)(2,1)}), bf16[256,2,512]{2,1,0:T(2,128)(2,1)S(1)}, u32[]{:S(2)}, u32[]{:S(2)}) async-start(bf16[256,2,512]{2,1,0:T(2,128)(2,1)} %bitcast.14), calls=%async_computation.1 | async-start | bytes 1048576 | tf_op jit(solution)/shard_map/all_to_all | solution.py:110

commit v2 on v1

v2 whole, which is shorter than its diff:
```python
import jax
import jax.numpy as jnp
from jax import lax
from jax.experimental import pallas as pl
from jax.experimental.pallas import tpu as pltpu
from jax.sharding import PartitionSpec as P

NEAR = [(0, 1), (1, 0), (2, 3), (3, 2)]
FAR = [(0, 2), (2, 0), (1, 3), (3, 1)]
HELD_FLOPS = 100_000_000_000


def held(array):
    def kernel(source, target):
        del source, target

    return pl.pallas_call(
        kernel,
        out_shape=jax.ShapeDtypeStruct(array.shape, array.dtype),
        in_specs=[pl.BlockSpec(memory_space=pl.ANY)],
        out_specs=pl.BlockSpec(memory_space=pl.ANY),
        input_output_aliases={0: 0},
        cost_estimate=pl.CostEstimate(flops=HELD_FLOPS, bytes_accessed=0, transcendentals=0),
        name="held",
    )(array)


def mirrored_groups(groups):
    def device(s, g, half, core):
        return ((s if half == 0 else 3 - s) * groups + g) * 4 + half * 2 + core

    return [
        [device(s, g, h, c) for g in range(groups) for h in range(2) for c in range(2)]
        for s in range(4)
    ]


def ranks_of(flat_ids, tokens):
    pair = jnp.arange(flat_ids.shape[0], dtype=jnp.int32)
    token = jnp.where(pair >= tokens, pair - tokens, pair)
    same = (flat_ids[:, None] == flat_ids[None, :]) & (token[:, None] < token[None, :])
    return jnp.sum(same.astype(jnp.int32), axis=0)


def body(upstream, expert_ids, gate_index, gate_table, w_up, w_down, saved_pre):
    tokens, model_width = upstream.shape
    col_part = model_width // lax.axis_size("section")
    groups = lax.axis_size("expert")
    experts = groups * lax.axis_size("dp")
    levels = gate_table.shape[0]
    capacity = saved_pre.shape[2]
    hidden_part = w_down.shape[1]
    section = lax.axis_index("section")
    half = lax.axis_index("dp") // 2
    first = section % 2 == 0
    kind = jnp.where(first, half, 1 - half)
    hidden_pair = section // 2

    flat_ids = expert_ids.T.reshape(-1)
    flat_index = gate_index.T.reshape(-1)
    ranks = ranks_of(flat_ids, tokens)
    gates = jnp.sum(
        jnp.where(
            flat_index[None, :] == jnp.arange(levels, dtype=jnp.int32)[:, None],
            gate_table[:, None],
            0.0,
        ),
        axis=0,
    )
    row = jnp.where(ranks == kind, flat_ids, -1)
    match = row[None, :] == jnp.arange(experts, dtype=jnp.int32)[:, None]
    row_gate = jnp.sum(jnp.where(match, gates[None, :], 0.0), axis=1)
    chosen = (match[:, :tokens] | match[:, tokens:]).astype(jnp.bfloat16)
    picked = jnp.dot(chosen, upstream, preferred_element_type=jnp.float32)
    rows = (row_gate[:, None] * picked).astype(jnp.bfloat16)
    arrived = lax.all_to_all(
        rows.reshape(experts, 2, model_width // 2),
        ("section", "expert", "dp"),
        split_axis=0,
        concat_axis=0,
        axis_index_groups=mirrored_groups(groups),
        tiled=True,
    ).reshape(experts, model_width)

    weight_own = w_down[0]
    weight_other = held(lax.ppermute(weight_own, "section", NEAR))
    pre = saved_pre[0].transpose(1, 2, 0)
    pre_mine = jnp.where(kind == 0, pre[0], pre[1])
    pre_other = lax.ppermute(jnp.where(kind == 0, pre[1], pre[0]), "section", NEAR)

    def hidden_grad(weight, pre_act):
        proj = jnp.einsum("fd,sd->fs", weight, arrived, preferred_element_type=jnp.float32)
        pre_act = pre_act.astype(jnp.float32)
        sig = jax.nn.sigmoid(pre_act)
        return (proj * (sig * (1.0 + pre_act * (1.0 - sig)))).astype(jnp.bfloat16)

    hid_own = hidden_grad(weight_own, pre_mine)
    far_own = lax.ppermute(hid_own, "section", FAR)
    near_own = lax.ppermute(hid_own, "section", NEAR)
    hid_other = hidden_grad(weight_other, pre_other)
    far_other = lax.ppermute(hid_other, "section", FAR)
    near_other = lax.ppermute(hid_other, "section", NEAR)
    relay_own = lax.ppermute(far_own, "section", NEAR)
    relay_other = lax.ppermute(far_other, "section", NEAR)

    pairs = w_up[0].reshape(col_part, 2, 2 * hidden_part)
    pairs = jnp.where(hidden_pair == 0, pairs, pairs[:, ::-1])
    parts = pairs.reshape(col_part, 2, 2, hidden_part)
    parts = jnp.where(first, parts, parts[:, :, ::-1]).reshape(col_part, 4 * hidden_part)

    def back(pieces):
        out = jnp.einsum(
            "fs,df->sd", jnp.concatenate(pieces), parts, preferred_element_type=jnp.float32
        )
        return out.astype(jnp.bfloat16)

    mine = back([hid_own, hid_other, far_own, far_other])
    theirs = back([near_other, near_own, relay_other, relay_own])
    back_rows = jnp.stack([mine, theirs], axis=1)
    returned = lax.all_to_all(
        back_rows, ("expert", "dp"), split_axis=0, concat_axis=0, tiled=True
    ).reshape(experts * capacity, col_part)

    sender_half = (flat_ids % 4) // 2
    served = jnp.where(first, sender_half, 1 - sender_half)
    places = flat_ids * capacity + jnp.where(ranks == served, 0, 1)
    wanted = places[:, None] == jnp.arange(experts * capacity, dtype=jnp.int32)
    wanted = (wanted[:tokens] | wanted[tokens:]).astype(jnp.bfloat16)
    total = jnp.dot(wanted, returned, preferred_element_type=jnp.float32)
    own_cols = lax.dynamic_slice_in_dim(upstream, section * col_part, col_part, 1)
    return (own_cols.astype(jnp.float32) + total).astype(jnp.bfloat16)


def solution(mesh):
    in_specs = (
        P(("expert", "dp"), None),
        P(("expert", "dp"), None),
        P(("expert", "dp"), None),
        P(),
        P(("expert", "dp"), "section", None),
        P(("expert", "dp"), "section", None),
        P(("expert", "dp"), None, None, "section"),
    )
    out_specs = P(("expert", "dp"), "section")
    return jax.shard_map(body, mesh=mesh, in_specs=in_specs, out_specs=out_specs, check_vma=False)
```

time: 172 us -> 148 us (0.86)
  starting transfers between devices: 76.2 us -> 64.5 us
  waiting for transfers between devices: 76.1 us -> 67.1 us
    ppermute x7 -> x8, waiting for transfers between devices: 28.5 us -> 14.1 us  [the longest x1 4.98 us: body(): far_other = lax.ppermute(hid_other, 'section', FAR)]
    all_to_all x1, starting transfers between devices: 21.4 us -> 8.84 us  [body(): lax.all_to_all(back_rows, ('expert', 'dp'), split_axis=0, concat_axis=0,...]
    all_to_all x1, waiting for transfers between devices: 22.7 us -> 28 us  [body(): lax.all_to_all(rows.reshape(experts, 2, model_width // 2), ('section', 'e...]
    ppermute x7 -> x8, starting transfers between devices: 25.8 us -> 25.9 us  [the longest x1 6.24 us: body(): far_other = lax.ppermute(hid_other, 'section', FAR)]
  transfers between devices with their start and end apart: 9 -> 10, of which waited for: 6 -> 7; matrix products, arithmetic and copies ran while one was open for 5% -> 7% of each run, Pallas kernels for 0% -> 0%
where the time goes in v2:
time: 148 us
  waiting for transfers between devices  67.1 us (45%)
  starting transfers between devices  64.5 us (44%)
  matrix products  7.01 us (5%)
  local copies, waits for them, and re-layouts  5.3 us (4%)
  other arithmetic  3.31 us (2%)
    all_to_all x1, starting transfers between devices, body(): lax.all_to_all(rows.reshape(experts, 2, model_width // 2), ('section', 'e...  29.8 us
    all_to_all x1, waiting for transfers between devices, body(): lax.all_to_all(rows.reshape(experts, 2, model_width // 2), ('section', 'e...  28 us
    all_to_all x1, waiting for transfers between devices, body(): lax.all_to_all(back_rows, ('expert', 'dp'), split_axis=0, concat_axis=0,...  25 us
    all_to_all x1, starting transfers between devices, body(): lax.all_to_all(back_rows, ('expert', 'dp'), split_axis=0, concat_axis=0,...  8.84 us
    ppermute x1, starting transfers between devices, body(): far_other = lax.ppermute(hid_other, 'section', FAR)  6.24 us
    ppermute x1, waiting for transfers between devices, body(): far_other = lax.ppermute(hid_other, 'section', FAR)  4.98 us
    ppermute x1, starting transfers between devices, body(): weight_other = held(lax.ppermute(weight_own, 'section', NEAR))  4.14 us
    ppermute x1, waiting for transfers between devices, body(): relay_other = lax.ppermute(far_other, 'section', NEAR)  3.86 us
  transfers between devices with their start and end apart: 10, of which 7 were waited for; matrix products, arithmetic and copies ran while one was open for 7% of the time, Pallas kernels for 0%

profile of v2, /device:TPU:1, one launch (start us, length us, event | category | flops | bytes accessed | tf_op | source)
XLA Modules:
  0.0 147.5 jit_solution(6411993775966187231)
XLA Ops:
  0.0 4.1 %collective-permute-start = (bf16[352,2048]{1,0:T(8,128)(2,1)}, bf16[352,2048]{1,0:T(8,128)(2,1)}, u32[]{:S(2)}, u32[]{:S(2)}) collective-permute-start(bf16[352,2048]{1,0:T(8,128)(2,1)} %bitcast.57), channel_id=1, source_target_pairs={{0,256},{256,0},{512,768},{768,512},{1,257},{257,1},{513,769},{769... | collective-permute-start | bytes 4325384 | tf_op jit(solution)/shard_map/ppermute | solution.py:86
  4.2 0.9 convert_reduce_fusion
  5.1 0.8 select_reduce_fusion.1
  6.8 1.5 fusion
  8.2 1.6 %reshape.102 = bf16[256,2,1024]{2,1,0:T(2,128)(2,1)} reshape(bf16[256,2048]{1,0:T(8,128)(2,1)S(1)} %fusion) | data formatting | bytes 2097152 | tf_op jit(solution)/shard_map/reshape | solution.py:77
  9.8 29.8 %all-to-all-start = ((bf16[256,2,1024]{2,1,0:T(2,128)(2,1)}), bf16[256,2,1024]{2,1,0:T(2,128)(2,1)}, u32[]{:S(2)}, u32[]{:S(2)}) async-start(bf16[256,2,1024]{2,1,0:T(2,128)(2,1)} %reshape.102), calls=%async_computation | async-start | bytes 2097152 | tf_op jit(solution)/shard_map/all_to_all | solution.py:76
  39.7 3.3 %collective-permute-start.1 = (bf16[352,256]{1,0:T(8,128)(2,1)S(1)}, bf16[352,256]{1,0:T(8,128)(2,1)}, u32[]{:S(2)}, u32[]{:S(2)}) collective-permute-start(bf16[352,256]{1,0:T(8,128)(2,1)S(1)} %select_bitcast_fusion), channel_id=1, source_target_pairs={{0,256},{256,0},{512,768},{768,512},{1,257},{257,1},{513,769},{769... | collective-permute-start | bytes 540680 | tf_op jit(solution)/shard_map/ppermute | solution.py:89
  44.0 28.0 %all-to-all-done = bf16[256,2,1024]{2,1,0:T(2,128)(2,1)} async-done(((bf16[256,2,1024]{2,1,0:T(2,128)(2,1)}), bf16[256,2,1024]{2,1,0:T(2,128)(2,1)}, u32[]{:S(2)}, u32[]{:S(2)}) %all-to-all-start) | async-done | bytes 1048608 | tf_op jit(solution)/shard_map/all_to_all | solution.py:76
  72.0 1.5 %copy.15 = bf16[32,8,2,1024]{3,1,2,0:T(8,128)(2,1)S(1)} copy(bf16[32,8,2,1024]{3,2,1,0:T(2,128)(2,1)} %bitcast.20) | data formatting | bytes 2097152
  74.1 1.9 %fusion.4 = bf16[352,256]{1,0:T(8,128)(2,1)S(1)} fusion(bf16[256,2048]{1,0:T(8,128)(2,1)S(1)} %bitcast.52, bf16[352,2048]{1,0:T(8,128)(2,1)} %held.1, bf16[352,256]{1,0:T(8,128)(2,1)} %collective-permute-done.1), kind=kOutput, calls=%fused_computation.11 | convolution fusion | flops 369999872 | bytes 2850816 | tf_op jit(solution)/shard_map/fd,sd->fs/dot_general | solution.py:92
  76.1 6.2 %collective-permute-start.3 = (bf16[352,256]{1,0:T(8,128)(2,1)S(1)}, bf16[352,256]{1,0:T(8,128)(2,1)S(1)}, u32[]{:S(2)}, u32[]{:S(2)}) collective-permute-start(bf16[352,256]{1,0:T(8,128)(2,1)S(1)} %fusion.4), channel_id=1, source_target_pairs={{0,512},{512,0},{256,768},{768,256},{1,513},{513,1},{257,769},{769... | collective-permute-start | bytes 540680 | tf_op jit(solution)/shard_map/ppermute | solution.py:101
  82.3 1.9 %collective-permute-start.2 = (bf16[352,256]{1,0:T(8,128)(2,1)S(1)}, bf16[352,256]{1,0:T(8,128)(2,1)S(1)}, u32[]{:S(2)}, u32[]{:S(2)}) collective-permute-start(bf16[352,256]{1,0:T(8,128)(2,1)S(1)} %fusion.3), channel_id=1, source_target_pairs={{0,512},{512,0},{256,768},{768,256},{1,513},{513,1},{257,769},{769... | collective-permute-start | bytes 540680 | tf_op jit(solution)/shard_map/ppermute | solution.py:98
  84.5 3.1 %collective-permute-start.4 = (bf16[352,256]{1,0:T(8,128)(2,1)S(1)}, bf16[352,256]{1,0:T(8,128)(2,1)S(1)}, u32[]{:S(2)}, u32[]{:S(2)}) collective-permute-start(bf16[352,256]{1,0:T(8,128)(2,1)S(1)} %fusion.4), channel_id=1, source_target_pairs={{0,256},{256,0},{512,768},{768,512},{1,257},{257,1},{513,769},{769... | collective-permute-start | bytes 540680 | tf_op jit(solution)/shard_map/ppermute | solution.py:102
  87.7 2.1 %collective-permute-start.5 = (bf16[352,256]{1,0:T(8,128)(2,1)S(1)}, bf16[352,256]{1,0:T(8,128)(2,1)S(1)}, u32[]{:S(2)}, u32[]{:S(2)}) collective-permute-start(bf16[352,256]{1,0:T(8,128)(2,1)S(1)} %fusion.3), channel_id=1, source_target_pairs={{0,256},{256,0},{512,768},{768,512},{1,257},{257,1},{513,769},{769... | collective-permute-start | bytes 540680 | tf_op jit(solution)/shard_map/ppermute | solution.py:99
  89.8 5.0 %collective-permute-done.3 = bf16[352,256]{1,0:T(8,128)(2,1)S(1)} collective-permute-done((bf16[352,256]{1,0:T(8,128)(2,1)S(1)}, bf16[352,256]{1,0:T(8,128)(2,1)S(1)}, u32[]{:S(2)}, u32[]{:S(2)}) %collective-permute-start.3) | collective-permute-done | bytes 180256 | tf_op jit(solution)/shard_map/ppermute | solution.py:101
  94.8 1.9 %collective-permute-start.6 = (bf16[352,256]{1,0:T(8,128)(2,1)S(1)}, bf16[352,256]{1,0:T(8,128)(2,1)S(1)}, u32[]{:S(2)}, u32[]{:S(2)}) collective-permute-start(bf16[352,256]{1,0:T(8,128)(2,1)S(1)} %collective-permute-done.3), channel_id=1, source_target_pairs={{0,256},{256,0},{512,768},{768,512},{1,257},{257,1},{513,769},{769... | collective-permute-start | bytes 540680 | tf_op jit(solution)/shard_map/ppermute | solution.py:104
  97.0 3.0 %collective-permute-start.7 = (bf16[352,256]{1,0:T(8,128)(2,1)S(1)}, bf16[352,256]{1,0:T(8,128)(2,1)S(1)}, u32[]{:S(2)}, u32[]{:S(2)}) collective-permute-start(bf16[352,256]{1,0:T(8,128)(2,1)S(1)} %collective-permute-done.2), channel_id=1, source_target_pairs={{0,256},{256,0},{512,768},{768,512},{1,257},{257,1},{513,769},{769... | collective-permute-start | bytes 540680 | tf_op jit(solution)/shard_map/ppermute | solution.py:103
  100.7 2.1 %collective-permute-done.5 = bf16[352,256]{1,0:T(8,128)(2,1)S(1)} collective-permute-done((bf16[352,256]{1,0:T(8,128)(2,1)S(1)}, bf16[352,256]{1,0:T(8,128)(2,1)S(1)}, u32[]{:S(2)}, u32[]{:S(2)}) %collective-permute-start.5) | collective-permute-done | bytes 180256 | tf_op jit(solution)/shard_map/ppermute | solution.py:99
  102.8 3.9 %collective-permute-done.6 = bf16[352,256]{1,0:T(8,128)(2,1)S(1)} collective-permute-done((bf16[352,256]{1,0:T(8,128)(2,1)S(1)}, bf16[352,256]{1,0:T(8,128)(2,1)S(1)}, u32[]{:S(2)}, u32[]{:S(2)}) %collective-permute-start.6) | collective-permute-done | bytes 180256 | tf_op jit(solution)/shard_map/ppermute | solution.py:104
  106.7 2.8 %collective-permute-done.7 = bf16[352,256]{1,0:T(8,128)(2,1)S(1)} collective-permute-done((bf16[352,256]{1,0:T(8,128)(2,1)S(1)}, bf16[352,256]{1,0:T(8,128)(2,1)S(1)}, u32[]{:S(2)}, u32[]{:S(2)}) %collective-permute-start.7) | collective-permute-done | bytes 180256 | tf_op jit(solution)/shard_map/ppermute | solution.py:103
  110.1 1.3 copy.14
  111.5 8.8 %all-to-all-start.1 = ((bf16[256,2,512]{2,1,0:T(2,128)(2,1)}), bf16[256,2,512]{2,1,0:T(2,128)(2,1)S(1)}, u32[]{:S(2)}, u32[]{:S(2)}) async-start(bf16[256,2,512]{2,1,0:T(2,128)(2,1)} %copy.14), calls=%async_computation.1 | async-start | bytes 1048576 | tf_op jit(solution)/shard_map/all_to_all | solution.py:120
  120.4 25.0 %all-to-all-done.1 = bf16[256,2,512]{2,1,0:T(2,128)(2,1)S(1)} async-done(((bf16[256,2,512]{2,1,0:T(2,128)(2,1)}), bf16[256,2,512]{2,1,0:T(2,128)(2,1)S(1)}, u32[]{:S(2)}, u32[]{:S(2)}) %all-to-all-start.1) | async-done | bytes 524320 | tf_op jit(solution)/shard_map/all_to_all | solution.py:120
  145.7 1.9 %fusion.7 = bf16[128,512]{1,0:T(8,128)(2,1)} fusion(bf16[512,512]{1,0:T(8,128)(2,1)S(1)} %reshape.106, pred[256,512]{1,0:T(32,128)(4,1)S(1)} %iota_compare_fusion, bf16[128,2048]{1,0:T(8,128)(2,1)} %param.7, s32[]{:T(128)S(6)} %select_n.118), kind=kOutput, calls=%fused_computation.15 | convolution fusion | flops 67371008 | bytes 917508 | tf_op jit(solution)/shard_map/dot_general | solution.py:129
  (25 shorter events, 4.6 us)
Async XLA Ops:
  0.0 44.0 %collective-permute-start = (bf16[352,2048]{1,0:T(8,128)(2,1)}, bf16[352,2048]{1,0:T(8,128)(2,1)}, u32[]{:S(2)}, u32[]{:S(2)}) collective-permute-start(bf16[352,2048]{1,0:T(8,128)(2,1)} %bitcast.57), channel_id=1, source_target_pairs={{0,256},{256,0},{512,768},{768,512},{1,257},{257,1},{513,769},{769... | collective-permute-start | bytes 4325384 | tf_op jit(solution)/shard_map/ppermute | solution.py:86
  9.8 29.8 %copy-start.1 = (bf16[1,256,2,352]{1,3,2,0:T(8,128)(2,1)S(1)}, bf16[1,256,2,352]{1,3,2,0:T(8,128)(2,1)}, u32[]{:S(2)}) copy-start(bf16[1,256,2,352]{1,3,2,0:T(8,128)(2,1)} %param.13) | copy-start | bytes 1081348
  9.8 33.2 %copy-start = (bf16[1,512,1408]{2,1,0:T(8,128)(2,1)S(1)}, bf16[1,512,1408]{2,1,0:T(8,128)(2,1)}, u32[]{:S(2)}) copy-start(bf16[1,512,1408]{2,1,0:T(8,128)(2,1)} %param.11) | copy-start | bytes 4325380
  9.8 62.2 %all-to-all-start = ((bf16[256,2,1024]{2,1,0:T(2,128)(2,1)}), bf16[256,2,1024]{2,1,0:T(2,128)(2,1)}, u32[]{:S(2)}, u32[]{:S(2)}) async-start(bf16[256,2,1024]{2,1,0:T(2,128)(2,1)} %reshape.102), calls=%async_computation | async-start | bytes 2097152 | tf_op jit(solution)/shard_map/all_to_all | solution.py:76
  39.7 34.5 %collective-permute-start.1 = (bf16[352,256]{1,0:T(8,128)(2,1)S(1)}, bf16[352,256]{1,0:T(8,128)(2,1)}, u32[]{:S(2)}, u32[]{:S(2)}) collective-permute-start(bf16[352,256]{1,0:T(8,128)(2,1)S(1)} %select_bitcast_fusion), channel_id=1, source_target_pairs={{0,256},{256,0},{512,768},{768,512},{1,257},{257,1},{513,769},{769... | collective-permute-start | bytes 540680 | tf_op jit(solution)/shard_map/ppermute | solution.py:89
  44.0 29.5 %copy-start.2 = (bf16[1,352,2048]{2,1,0:T(8,128)(2,1)S(1)}, bf16[1,352,2048]{2,1,0:T(8,128)(2,1)}, u32[]{:S(2)}) copy-start(bf16[1,352,2048]{2,1,0:T(8,128)(2,1)} %param.12) | copy-start | bytes 4325380
  76.1 18.7 %collective-permute-start.3 = (bf16[352,256]{1,0:T(8,128)(2,1)S(1)}, bf16[352,256]{1,0:T(8,128)(2,1)S(1)}, u32[]{:S(2)}, u32[]{:S(2)}) collective-permute-start(bf16[352,256]{1,0:T(8,128)(2,1)S(1)} %fusion.4), channel_id=1, source_target_pairs={{0,512},{512,0},{256,768},{768,256},{1,513},{513,1},{257,769},{769... | collective-permute-start | bytes 540680 | tf_op jit(solution)/shard_map/ppermute | solution.py:101
  82.3 14.7 %collective-permute-start.2 = (bf16[352,256]{1,0:T(8,128)(2,1)S(1)}, bf16[352,256]{1,0:T(8,128)(2,1)S(1)}, u32[]{:S(2)}, u32[]{:S(2)}) collective-permute-start(bf16[352,256]{1,0:T(8,128)(2,1)S(1)} %fusion.3), channel_id=1, source_target_pairs={{0,512},{512,0},{256,768},{768,256},{1,513},{513,1},{257,769},{769... | collective-permute-start | bytes 540680 | tf_op jit(solution)/shard_map/ppermute | solution.py:98
  84.5 16.2 %collective-permute-start.4 = (bf16[352,256]{1,0:T(8,128)(2,1)S(1)}, bf16[352,256]{1,0:T(8,128)(2,1)S(1)}, u32[]{:S(2)}, u32[]{:S(2)}) collective-permute-start(bf16[352,256]{1,0:T(8,128)(2,1)S(1)} %fusion.4), channel_id=1, source_target_pairs={{0,256},{256,0},{512,768},{768,512},{1,257},{257,1},{513,769},{769... | collective-permute-start | bytes 540680 | tf_op jit(solution)/shard_map/ppermute | solution.py:102
  87.7 15.2 %collective-permute-start.5 = (bf16[352,256]{1,0:T(8,128)(2,1)S(1)}, bf16[352,256]{1,0:T(8,128)(2,1)S(1)}, u32[]{:S(2)}, u32[]{:S(2)}) collective-permute-start(bf16[352,256]{1,0:T(8,128)(2,1)S(1)} %fusion.3), channel_id=1, source_target_pairs={{0,256},{256,0},{512,768},{768,512},{1,257},{257,1},{513,769},{769... | collective-permute-start | bytes 540680 | tf_op jit(solution)/shard_map/ppermute | solution.py:99
  94.8 11.9 %collective-permute-start.6 = (bf16[352,256]{1,0:T(8,128)(2,1)S(1)}, bf16[352,256]{1,0:T(8,128)(2,1)S(1)}, u32[]{:S(2)}, u32[]{:S(2)}) collective-permute-start(bf16[352,256]{1,0:T(8,128)(2,1)S(1)} %collective-permute-done.3), channel_id=1, source_target_pairs={{0,256},{256,0},{512,768},{768,512},{1,257},{257,1},{513,769},{769... | collective-permute-start | bytes 540680 | tf_op jit(solution)/shard_map/ppermute | solution.py:104
  97.0 12.4 %collective-permute-start.7 = (bf16[352,256]{1,0:T(8,128)(2,1)S(1)}, bf16[352,256]{1,0:T(8,128)(2,1)S(1)}, u32[]{:S(2)}, u32[]{:S(2)}) collective-permute-start(bf16[352,256]{1,0:T(8,128)(2,1)S(1)} %collective-permute-done.2), channel_id=1, source_target_pairs={{0,256},{256,0},{512,768},{768,512},{1,257},{257,1},{513,769},{769... | collective-permute-start | bytes 540680 | tf_op jit(solution)/shard_map/ppermute | solution.py:103
  111.5 34.0 %all-to-all-start.1 = ((bf16[256,2,512]{2,1,0:T(2,128)(2,1)}), bf16[256,2,512]{2,1,0:T(2,128)(2,1)S(1)}, u32[]{:S(2)}, u32[]{:S(2)}) async-start(bf16[256,2,512]{2,1,0:T(2,128)(2,1)} %copy.14), calls=%async_computation.1 | async-start | bytes 1048576 | tf_op jit(solution)/shard_map/all_to_all | solution.py:120

commit v3 on v2

--- a/solution.py
+++ b/solution.py
@@ -10,17 +10,19 @@
 HELD_FLOPS = 100_000_000_000
 
 
-def held(array):
-    def kernel(source, target):
-        del source, target
+def held(array, flops):
+    def kernel(*refs):
+        del refs
 
+    anywhere = pl.BlockSpec(memory_space=pl.ANY)
     return pl.pallas_call(
         kernel,
         out_shape=jax.ShapeDtypeStruct(array.shape, array.dtype),
-        in_specs=[pl.BlockSpec(memory_space=pl.ANY)],
-        out_specs=pl.BlockSpec(memory_space=pl.ANY),
+        in_specs=[anywhere],
+        out_specs=anywhere,
         input_output_aliases={0: 0},
-        cost_estimate=pl.CostEstimate(flops=HELD_FLOPS, bytes_accessed=0, transcendentals=0),
+        cost_estimate=pl.CostEstimate(flops=flops, bytes_accessed=0, transcendentals=0),
+        compiler_params=pltpu.CompilerParams(vmem_limit_bytes=1 << 17),
         name="held",
     )(array)
 
@@ -35,6 +37,68 @@
     ]
 
 
+def gated_rows_kernel(kind_ref, table_ref, ids_ref, index_ref, up_ref, out_ref):
+    experts, tokens = out_ref.shape[0], up_ref.shape[0]
+    width = out_ref.shape[2]
+    ids, index = ids_ref[...], index_ref[...]
+    expert = lax.broadcasted_iota(jnp.int32, (experts, tokens), 0)
+    named = [ids[k : k + 1] == expert for k in range(2)]
+    either = jnp.where(named[0] | named[1], 1.0, 0.0)
+    before = lax.broadcasted_iota(jnp.int32, (tokens, tokens), 0) < lax.broadcasted_iota(
+        jnp.int32, (tokens, tokens), 1
+    )
+    before = jnp.where(before, 1.0, 0.0).astype(jnp.bfloat16)
+    earlier = jnp.dot(either.astype(jnp.bfloat16), before, preferred_element_type=jnp.float32)
+    here = jnp.where(earlier == kind_ref[0].astype(jnp.float32), either, 0.0)
+    gates = jnp.zeros(index.shape, jnp.float32)
+    for level in range(table_ref.shape[0]):
+        gates = jnp.where(index == level, table_ref[level], gates)
+    gate = jnp.where(named[0], gates[0:1], gates[1:2]) * here
+    row_gate = jnp.sum(gate, axis=1, keepdims=True)
+    picked = jnp.dot(here.astype(jnp.bfloat16), up_ref[...], preferred_element_type=jnp.float32)
+    rows = (row_gate * picked).astype(jnp.bfloat16)
+    out_ref[:, 0, :] = rows[:, :width]
+    out_ref[:, 1, :] = rows[:, width:]
+
+
+def gated_rows(kind, table, ids, index, upstream, experts):
+    smem = pl.BlockSpec(memory_space=pltpu.SMEM)
+    vmem = pl.BlockSpec(memory_space=pltpu.VMEM)
+    return pl.pallas_call(
+        gated_rows_kernel,
+        out_shape=jax.ShapeDtypeStruct((experts, 2, upstream.shape[1] // 2), jnp.bfloat16),
+        in_specs=[smem, smem, vmem, vmem, vmem],
+        out_specs=vmem,
+        compiler_params=pltpu.CompilerParams(vmem_limit_bytes=8 << 20),
+        name="gated_rows",
+    )(kind.reshape(1), table, ids, index, upstream)
+
+
+def reorder_kernel(section_ref, w_ref, after_ref, out_ref):
+    del after_ref
+    flipped = w_ref[...].T
+    part = flipped.shape[0] // 4
+    for j in range(4):
+        to = pl.multiple_of(jnp.bitwise_xor(section_ref[0], j) * part, 32)
+        out_ref[pl.ds(to, part), :] = flipped[j * part : (j + 1) * part]
+
+
+def reorder(section, w, after):
+    vmem = pl.BlockSpec(memory_space=pltpu.VMEM)
+    return pl.pallas_call(
+        reorder_kernel,
+        out_shape=jax.ShapeDtypeStruct(w.shape[::-1], w.dtype),
+        in_specs=[
+            pl.BlockSpec(memory_space=pltpu.SMEM),
+            vmem,
+            pl.BlockSpec(memory_space=pl.ANY),
+        ],
+        out_specs=vmem,
+        compiler_params=pltpu.CompilerParams(vmem_limit_bytes=8 << 20),
+        name="reorder",
+    )(section.reshape(1), w, after)
+
+
 def ranks_of(flat_ids, tokens):
     pair = jnp.arange(flat_ids.shape[0], dtype=jnp.int32)
     token = jnp.where(pair >= tokens, pair - tokens, pair)
@@ -47,34 +111,17 @@
     col_part = model_width // lax.axis_size("section")
     groups = lax.axis_size("expert")
     experts = groups * lax.axis_size("dp")
-    levels = gate_table.shape[0]
     capacity = saved_pre.shape[2]
-    hidden_part = w_down.shape[1]
     section = lax.axis_index("section")
     half = lax.axis_index("dp") // 2
     first = section % 2 == 0
     kind = jnp.where(first, half, 1 - half)
-    hidden_pair = section // 2
 
     flat_ids = expert_ids.T.reshape(-1)
-    flat_index = gate_index.T.reshape(-1)
     ranks = ranks_of(flat_ids, tokens)
-    gates = jnp.sum(
-        jnp.where(
-            flat_index[None, :] == jnp.arange(levels, dtype=jnp.int32)[:, None],
-            gate_table[:, None],
-            0.0,
-        ),
-        axis=0,
-    )
-    row = jnp.where(ranks == kind, flat_ids, -1)
-    match = row[None, :] == jnp.arange(experts, dtype=jnp.int32)[:, None]
-    row_gate = jnp.sum(jnp.where(match, gates[None, :], 0.0), axis=1)
-    chosen = (match[:, :tokens] | match[:, tokens:]).astype(jnp.bfloat16)
-    picked = jnp.dot(chosen, upstream, preferred_element_type=jnp.float32)
-    rows = (row_gate[:, None] * picked).astype(jnp.bfloat16)
+    rows = gated_rows(kind, gate_table, expert_ids.T, gate_index.T, upstream, experts)
     arrived = lax.all_to_all(
-        rows.reshape(experts, 2, model_width // 2),
+        rows,
         ("section", "expert", "dp"),
         split_axis=0,
         concat_axis=0,
@@ -83,7 +130,7 @@
     ).reshape(experts, model_width)
 
     weight_own = w_down[0]
-    weight_other = held(lax.ppermute(weight_own, "section", NEAR))
+    weight_other = held(lax.ppermute(weight_own, "section", NEAR), HELD_FLOPS)
     pre = saved_pre[0].transpose(1, 2, 0)
     pre_mine = jnp.where(kind == 0, pre[0], pre[1])
     pre_other = lax.ppermute(jnp.where(kind == 0, pre[1], pre[0]), "section", NEAR)
@@ -103,14 +150,11 @@
     relay_own = lax.ppermute(far_own, "section", NEAR)
     relay_other = lax.ppermute(far_other, "section", NEAR)
 
-    pairs = w_up[0].reshape(col_part, 2, 2 * hidden_part)
-    pairs = jnp.where(hidden_pair == 0, pairs, pairs[:, ::-1])
-    parts = pairs.reshape(col_part, 2, 2, hidden_part)
-    parts = jnp.where(first, parts, parts[:, :, ::-1]).reshape(col_part, 4 * hidden_part)
+    parts = reorder(section, w_up[0], hid_own)
 
     def back(pieces):
         out = jnp.einsum(
-            "fs,df->sd", jnp.concatenate(pieces), parts, preferred_element_type=jnp.float32
+            "fs,fd->sd", jnp.concatenate(pieces), parts, preferred_element_type=jnp.float32
         )
         return out.astype(jnp.bfloat16)
 

time: 148 us -> 145 us (0.980)
  other arithmetic: 3.31 us -> 0.39 us
  matrix products: 7.01 us -> 4.17 us
  Pallas kernels: 0.01 us -> 2.74 us
    pallas_call x0 -> x2, Pallas kernels: none -> 2.73 us  [the longest x1 2.29 us: gated_rows(): pl.pallas_call(gated_rows_kernel, out_shape=jax.ShapeDtypeStruct((experts...]
    all_to_all x1, waiting for transfers between devices: 28 us -> 29.9 us  [body(): lax.all_to_all(rows, ('section', 'expert', 'dp'), split_axis=0, concat_ax...]
    reshape x1 -> x0, local copies, waits for them, and re-layouts: 1.58 us -> none  [body(): rows.reshape(experts, 2, model_width // 2)]
    unnamed x8 -> x17, local copies, waits for them, and re-layouts: 2.2 us -> 3.34 us
  transfers between devices with their start and end apart: 10 -> 10, of which waited for: 7 -> 7; matrix products, arithmetic and copies ran while one was open for 7% -> 1% of each run, Pallas kernels for 0% -> 2%
where the time goes in v3:
time: 145 us
  waiting for transfers between devices  68.3 us (47%)
  starting transfers between devices  64.1 us (44%)
  local copies, waits for them, and re-layouts  4.86 us (3%)
  matrix products  4.17 us (3%)
  Pallas kernels  2.74 us (2%)
    all_to_all x1, waiting for transfers between devices, body(): lax.all_to_all(rows, ('section', 'expert', 'dp'), split_axis=0, concat_ax...  29.9 us
    all_to_all x1, starting transfers between devices, body(): lax.all_to_all(rows, ('section', 'expert', 'dp'), split_axis=0, concat_ax...  28.8 us
    all_to_all x1, waiting for transfers between devices, body(): lax.all_to_all(back_rows, ('expert', 'dp'), split_axis=0, concat_axis=0,...  24.8 us
    all_to_all x1, starting transfers between devices, body(): lax.all_to_all(back_rows, ('expert', 'dp'), split_axis=0, concat_axis=0,...  9.31 us
    ppermute x1, starting transfers between devices, body(): far_other = lax.ppermute(hid_other, 'section', FAR)  6.37 us
    ppermute x1, waiting for transfers between devices, body(): far_other = lax.ppermute(hid_other, 'section', FAR)  4.2 us
    ppermute x1, starting transfers between devices, body(): weight_other = held(lax.ppermute(weight_own, 'section', NEAR), HELD_FLOPS)  4.14 us
    ppermute x1, waiting for transfers between devices, body(): relay_other = lax.ppermute(far_other, 'section', NEAR)  3.86 us
  transfers between devices with their start and end apart: 10, of which 7 were waited for; matrix products, arithmetic and copies ran while one was open for 1% of the time, Pallas kernels for 2%

profile of v3, /device:TPU:1, one launch (start us, length us, event | category | flops | bytes accessed | tf_op | source)
XLA Modules:
  0.0 144.9 jit_solution(17112507425647156722)
XLA Ops:
  0.0 4.1 %collective-permute-start = (bf16[352,2048]{1,0:T(8,128)(2,1)}, bf16[352,2048]{1,0:T(8,128)(2,1)S(1)}, u32[]{:S(2)}, u32[]{:S(2)}) collective-permute-start(bf16[352,2048]{1,0:T(8,128)(2,1)} %bitcast.52), channel_id=1, source_target_pairs={{0,256},{256,0},{512,768},{768,512},{1,257},{257,1},{513,769},{769... | collective-permute-start | bytes 4325384 | tf_op jit(solution)/shard_map/ppermute | solution.py:133
  4.2 1.0 copy-done.1
  5.2 0.7 copy-done.2
  5.9 0.7 copy-done.4
  6.6 0.7 copy-done.5
  7.2 2.3 %gated_rows.1 = bf16[256,2,1024]{2,1,0:T(2,128)(2,1)} custom-call(s32[1]{0:T(128)} %bitcast.3.kind_ref, f32[64]{0:T(128)S(1)} %copy-done.5, s32[2,128]{1,0:T(2,128)S(1)} %bitcast.44, s32[2,128]{1,0:T(2,128)S(1)} %bitcast.46, bf16[128,2048]{1,0:T(8,128)(2,1)S(1)} %copy-done.1), custom_call_target="tpu_custom_call" | custom-call | tf_op jit(solution)/shard_map/gated_rows/pallas_call | solution.py:67
  9.5 28.8 %all-to-all-start = ((bf16[256,2,1024]{2,1,0:T(2,128)(2,1)}), bf16[256,2,1024]{2,1,0:T(2,128)(2,1)S(1)}, u32[]{:S(2)}, u32[]{:S(2)}) async-start(bf16[256,2,1024]{2,1,0:T(2,128)(2,1)} %gated_rows.1), calls=%async_computation | async-start | bytes 2097152 | tf_op jit(solution)/shard_map/all_to_all | solution.py:123
  38.4 3.3 %collective-permute-start.1 = (bf16[352,256]{1,0:T(8,128)(2,1)S(1)}, bf16[352,256]{1,0:T(8,128)(2,1)S(1)}, u32[]{:S(2)}, u32[]{:S(2)}) collective-permute-start(bf16[352,256]{1,0:T(8,128)(2,1)S(1)} %select_bitcast_fusion), channel_id=1, source_target_pairs={{0,256},{256,0},{512,768},{768,512},{1,257},{257,1},{513,769},{769... | collective-permute-start | bytes 540680 | tf_op jit(solution)/shard_map/ppermute | solution.py:136
  41.7 29.9 %all-to-all-done = bf16[256,2,1024]{2,1,0:T(2,128)(2,1)S(1)} async-done(((bf16[256,2,1024]{2,1,0:T(2,128)(2,1)}), bf16[256,2,1024]{2,1,0:T(2,128)(2,1)S(1)}, u32[]{:S(2)}, u32[]{:S(2)}) %all-to-all-start) | async-done | bytes 1048608 | tf_op jit(solution)/shard_map/all_to_all | solution.py:123
  72.5 6.4 %collective-permute-start.3 = (bf16[352,256]{1,0:T(8,128)(2,1)S(1)}, bf16[352,256]{1,0:T(8,128)(2,1)S(1)}, u32[]{:S(2)}, u32[]{:S(2)}) collective-permute-start(bf16[352,256]{1,0:T(8,128)(2,1)S(1)} %fusion.3), channel_id=1, source_target_pairs={{0,512},{512,0},{256,768},{768,256},{1,513},{513,1},{257,769},{769... | collective-permute-start | bytes 540680 | tf_op jit(solution)/shard_map/ppermute | solution.py:148
  79.5 1.9 %collective-permute-start.2 = (bf16[352,256]{1,0:T(8,128)(2,1)S(1)}, bf16[352,256]{1,0:T(8,128)(2,1)S(1)}, u32[]{:S(2)}, u32[]{:S(2)}) collective-permute-start(bf16[352,256]{1,0:T(8,128)(2,1)S(1)} %fusion.2.after_ref), channel_id=1, source_target_pairs={{0,512},{512,0},{256,768},{768,256},{1,513},{513,1},{257,769},{769... | collective-permute-start | bytes 540680 | tf_op jit(solution)/shard_map/ppermute | solution.py:145
  81.4 3.1 %collective-permute-start.4 = (bf16[352,256]{1,0:T(8,128)(2,1)S(1)}, bf16[352,256]{1,0:T(8,128)(2,1)S(1)}, u32[]{:S(2)}, u32[]{:S(2)}) collective-permute-start(bf16[352,256]{1,0:T(8,128)(2,1)S(1)} %fusion.3), channel_id=1, source_target_pairs={{0,256},{256,0},{512,768},{768,512},{1,257},{257,1},{513,769},{769... | collective-permute-start | bytes 540680 | tf_op jit(solution)/shard_map/ppermute | solution.py:149
  84.6 2.1 %collective-permute-start.5 = (bf16[352,256]{1,0:T(8,128)(2,1)S(1)}, bf16[352,256]{1,0:T(8,128)(2,1)S(1)}, u32[]{:S(2)}, u32[]{:S(2)}) collective-permute-start(bf16[352,256]{1,0:T(8,128)(2,1)S(1)} %fusion.2.after_ref), channel_id=1, source_target_pairs={{0,256},{256,0},{512,768},{768,512},{1,257},{257,1},{513,769},{769... | collective-permute-start | bytes 540680 | tf_op jit(solution)/shard_map/ppermute | solution.py:146
  87.2 4.2 %collective-permute-done.3 = bf16[352,256]{1,0:T(8,128)(2,1)S(1)} collective-permute-done((bf16[352,256]{1,0:T(8,128)(2,1)S(1)}, bf16[352,256]{1,0:T(8,128)(2,1)S(1)}, u32[]{:S(2)}, u32[]{:S(2)}) %collective-permute-start.3) | collective-permute-done | bytes 180256 | tf_op jit(solution)/shard_map/ppermute | solution.py:148
  91.4 1.9 %collective-permute-start.6 = (bf16[352,256]{1,0:T(8,128)(2,1)S(1)}, bf16[352,256]{1,0:T(8,128)(2,1)S(1)}, u32[]{:S(2)}, u32[]{:S(2)}) collective-permute-start(bf16[352,256]{1,0:T(8,128)(2,1)S(1)} %collective-permute-done.3), channel_id=1, source_target_pairs={{0,256},{256,0},{512,768},{768,512},{1,257},{257,1},{513,769},{769... | collective-permute-start | bytes 540680 | tf_op jit(solution)/shard_map/ppermute | solution.py:151
  93.6 3.0 %collective-permute-start.7 = (bf16[352,256]{1,0:T(8,128)(2,1)S(1)}, bf16[352,256]{1,0:T(8,128)(2,1)S(1)}, u32[]{:S(2)}, u32[]{:S(2)}) collective-permute-start(bf16[352,256]{1,0:T(8,128)(2,1)S(1)} %collective-permute-done.2), channel_id=1, source_target_pairs={{0,256},{256,0},{512,768},{768,512},{1,257},{257,1},{513,769},{769... | collective-permute-start | bytes 540680 | tf_op jit(solution)/shard_map/ppermute | solution.py:150
  96.7 0.6 fusion.4
  97.3 2.7 %collective-permute-done.5 = bf16[352,256]{1,0:T(8,128)(2,1)S(1)} collective-permute-done((bf16[352,256]{1,0:T(8,128)(2,1)S(1)}, bf16[352,256]{1,0:T(8,128)(2,1)S(1)}, u32[]{:S(2)}, u32[]{:S(2)}) %collective-permute-start.5) | collective-permute-done | bytes 180256 | tf_op jit(solution)/shard_map/ppermute | solution.py:146
  100.0 3.9 %collective-permute-done.6 = bf16[352,256]{1,0:T(8,128)(2,1)S(1)} collective-permute-done((bf16[352,256]{1,0:T(8,128)(2,1)S(1)}, bf16[352,256]{1,0:T(8,128)(2,1)S(1)}, u32[]{:S(2)}, u32[]{:S(2)}) %collective-permute-start.6) | collective-permute-done | bytes 180256 | tf_op jit(solution)/shard_map/ppermute | solution.py:151
  103.9 2.5 %collective-permute-done.7 = bf16[352,256]{1,0:T(8,128)(2,1)S(1)} collective-permute-done((bf16[352,256]{1,0:T(8,128)(2,1)S(1)}, bf16[352,256]{1,0:T(8,128)(2,1)S(1)}, u32[]{:S(2)}, u32[]{:S(2)}) %collective-permute-start.7) | collective-permute-done | bytes 180256 | tf_op jit(solution)/shard_map/ppermute | solution.py:150
  107.0 1.3 copy.11
  108.4 9.3 %all-to-all-start.1 = ((bf16[256,2,512]{2,1,0:T(2,128)(2,1)}), bf16[256,2,512]{2,1,0:T(2,128)(2,1)S(1)}, u32[]{:S(2)}, u32[]{:S(2)}) async-start(bf16[256,2,512]{2,1,0:T(2,128)(2,1)} %copy.11), calls=%async_computation.1 | async-start | bytes 1048576 | tf_op jit(solution)/shard_map/all_to_all | solution.py:164
  118.0 24.8 %all-to-all-done.1 = bf16[256,2,512]{2,1,0:T(2,128)(2,1)S(1)} async-done(((bf16[256,2,512]{2,1,0:T(2,128)(2,1)}), bf16[256,2,512]{2,1,0:T(2,128)(2,1)S(1)}, u32[]{:S(2)}, u32[]{:S(2)}) %all-to-all-start.1) | async-done | bytes 524320 | tf_op jit(solution)/shard_map/all_to_all | solution.py:164
  143.0 1.8 %fusion.6 = bf16[128,512]{1,0:T(8,128)(2,1)} fusion(bf16[512,512]{1,0:T(8,128)(2,1)S(1)} %reshape.90, pred[256,512]{1,0:T(32,128)(4,1)S(1)} %iota_compare_fusion, bf16[128,2048]{1,0:T(8,128)(2,1)} %up_ref.1, s32[]{:T(128)S(6)} %select_n.83), kind=kOutput, calls=%fused_computation.11 | convolution fusion | flops 67371008 | bytes 917508 | tf_op jit(solution)/shard_map/dot_general | solution.py:173
  (29 shorter events, 3.4 us)
Async XLA Ops:
  0.0 41.7 %collective-permute-start = (bf16[352,2048]{1,0:T(8,128)(2,1)}, bf16[352,2048]{1,0:T(8,128)(2,1)S(1)}, u32[]{:S(2)}, u32[]{:S(2)}) collective-permute-start(bf16[352,2048]{1,0:T(8,128)(2,1)} %bitcast.52), channel_id=1, source_target_pairs={{0,256},{256,0},{512,768},{768,512},{1,257},{257,1},{513,769},{769... | collective-permute-start | bytes 4325384 | tf_op jit(solution)/shard_map/ppermute | solution.py:133
  4.2 1.0 copy-start.1
  5.2 0.7 copy-start.2
  5.9 0.7 copy-start.4
  6.6 0.7 copy-start.5
  9.5 28.8 %copy-start.6 = (bf16[1,256,2,352]{1,3,2,0:T(8,128)(2,1)S(1)}, bf16[1,256,2,352]{1,3,2,0:T(8,128)(2,1)}, u32[]{:S(2)}) copy-start(bf16[1,256,2,352]{1,3,2,0:T(8,128)(2,1)} %param.13) | copy-start | bytes 1081348
  9.5 62.1 %all-to-all-start = ((bf16[256,2,1024]{2,1,0:T(2,128)(2,1)}), bf16[256,2,1024]{2,1,0:T(2,128)(2,1)S(1)}, u32[]{:S(2)}, u32[]{:S(2)}) async-start(bf16[256,2,1024]{2,1,0:T(2,128)(2,1)} %gated_rows.1), calls=%async_computation | async-start | bytes 2097152 | tf_op jit(solution)/shard_map/all_to_all | solution.py:123
  38.4 33.5 %collective-permute-start.1 = (bf16[352,256]{1,0:T(8,128)(2,1)S(1)}, bf16[352,256]{1,0:T(8,128)(2,1)S(1)}, u32[]{:S(2)}, u32[]{:S(2)}) collective-permute-start(bf16[352,256]{1,0:T(8,128)(2,1)S(1)} %select_bitcast_fusion), channel_id=1, source_target_pairs={{0,256},{256,0},{512,768},{768,512},{1,257},{257,1},{513,769},{769... | collective-permute-start | bytes 540680 | tf_op jit(solution)/shard_map/ppermute | solution.py:136
  71.9 7.0 %copy-start.7 = (bf16[1,352,2048]{2,1,0:T(8,128)(2,1)S(1)}, bf16[1,352,2048]{2,1,0:T(8,128)(2,1)}, u32[]{:S(2)}) copy-start(bf16[1,352,2048]{2,1,0:T(8,128)(2,1)} %param.12) | copy-start | bytes 4325380
  72.5 14.2 %copy-start = (bf16[1,512,1408]{2,1,0:T(8,128)(2,1)S(1)}, bf16[1,512,1408]{2,1,0:T(8,128)(2,1)}, u32[]{:S(2)}) copy-start(bf16[1,512,1408]{2,1,0:T(8,128)(2,1)} %param.11) | copy-start | bytes 4325380
  72.5 18.9 %collective-permute-start.3 = (bf16[352,256]{1,0:T(8,128)(2,1)S(1)}, bf16[352,256]{1,0:T(8,128)(2,1)S(1)}, u32[]{:S(2)}, u32[]{:S(2)}) collective-permute-start(bf16[352,256]{1,0:T(8,128)(2,1)S(1)} %fusion.3), channel_id=1, source_target_pairs={{0,512},{512,0},{256,768},{768,256},{1,513},{513,1},{257,769},{769... | collective-permute-start | bytes 540680 | tf_op jit(solution)/shard_map/ppermute | solution.py:148
  79.5 14.1 %collective-permute-start.2 = (bf16[352,256]{1,0:T(8,128)(2,1)S(1)}, bf16[352,256]{1,0:T(8,128)(2,1)S(1)}, u32[]{:S(2)}, u32[]{:S(2)}) collective-permute-start(bf16[352,256]{1,0:T(8,128)(2,1)S(1)} %fusion.2.after_ref), channel_id=1, source_target_pairs={{0,512},{512,0},{256,768},{768,256},{1,513},{513,1},{257,769},{769... | collective-permute-start | bytes 540680 | tf_op jit(solution)/shard_map/ppermute | solution.py:145
  81.4 15.9 %collective-permute-start.4 = (bf16[352,256]{1,0:T(8,128)(2,1)S(1)}, bf16[352,256]{1,0:T(8,128)(2,1)S(1)}, u32[]{:S(2)}, u32[]{:S(2)}) collective-permute-start(bf16[352,256]{1,0:T(8,128)(2,1)S(1)} %fusion.3), channel_id=1, source_target_pairs={{0,256},{256,0},{512,768},{768,512},{1,257},{257,1},{513,769},{769... | collective-permute-start | bytes 540680 | tf_op jit(solution)/shard_map/ppermute | solution.py:149
  84.6 15.5 %collective-permute-start.5 = (bf16[352,256]{1,0:T(8,128)(2,1)S(1)}, bf16[352,256]{1,0:T(8,128)(2,1)S(1)}, u32[]{:S(2)}, u32[]{:S(2)}) collective-permute-start(bf16[352,256]{1,0:T(8,128)(2,1)S(1)} %fusion.2.after_ref), channel_id=1, source_target_pairs={{0,256},{256,0},{512,768},{768,512},{1,257},{257,1},{513,769},{769... | collective-permute-start | bytes 540680 | tf_op jit(solution)/shard_map/ppermute | solution.py:146
  91.4 12.5 %collective-permute-start.6 = (bf16[352,256]{1,0:T(8,128)(2,1)S(1)}, bf16[352,256]{1,0:T(8,128)(2,1)S(1)}, u32[]{:S(2)}, u32[]{:S(2)}) collective-permute-start(bf16[352,256]{1,0:T(8,128)(2,1)S(1)} %collective-permute-done.3), channel_id=1, source_target_pairs={{0,256},{256,0},{512,768},{768,512},{1,257},{257,1},{513,769},{769... | collective-permute-start | bytes 540680 | tf_op jit(solution)/shard_map/ppermute | solution.py:151
  93.6 12.7 %collective-permute-start.7 = (bf16[352,256]{1,0:T(8,128)(2,1)S(1)}, bf16[352,256]{1,0:T(8,128)(2,1)S(1)}, u32[]{:S(2)}, u32[]{:S(2)}) collective-permute-start(bf16[352,256]{1,0:T(8,128)(2,1)S(1)} %collective-permute-done.2), channel_id=1, source_target_pairs={{0,256},{256,0},{512,768},{768,512},{1,257},{257,1},{513,769},{769... | collective-permute-start | bytes 540680 | tf_op jit(solution)/shard_map/ppermute | solution.py:150
  106.9 10.7 %copy-start.3 = (s32[128,2]{0,1:T(2,128)S(1)}, s32[128,2]{0,1:T(2,128)}, u32[]{:S(2)}) copy-start(s32[128,2]{0,1:T(2,128)} %param.8) | copy-start | bytes 3076
  108.4 34.5 %all-to-all-start.1 = ((bf16[256,2,512]{2,1,0:T(2,128)(2,1)}), bf16[256,2,512]{2,1,0:T(2,128)(2,1)S(1)}, u32[]{:S(2)}, u32[]{:S(2)}) async-start(bf16[256,2,512]{2,1,0:T(2,128)(2,1)} %copy.11), calls=%async_computation.1 | async-start | bytes 1048576 | tf_op jit(solution)/shard_map/all_to_all | solution.py:164

commit v4 on v3

--- a/solution.py
+++ b/solution.py
@@ -8,6 +8,7 @@
 NEAR = [(0, 1), (1, 0), (2, 3), (3, 2)]
 FAR = [(0, 2), (2, 0), (1, 3), (3, 1)]
 HELD_FLOPS = 100_000_000_000
+ROWS_VMEM = 65_200_000
 
 
 def held(array, flops):
@@ -69,7 +70,7 @@
         out_shape=jax.ShapeDtypeStruct((experts, 2, upstream.shape[1] // 2), jnp.bfloat16),
         in_specs=[smem, smem, vmem, vmem, vmem],
         out_specs=vmem,
-        compiler_params=pltpu.CompilerParams(vmem_limit_bytes=8 << 20),
+        compiler_params=pltpu.CompilerParams(vmem_limit_bytes=ROWS_VMEM),
         name="gated_rows",
     )(kind.reshape(1), table, ids, index, upstream)
 
@@ -143,10 +144,9 @@
 
     hid_own = hidden_grad(weight_own, pre_mine)
     far_own = lax.ppermute(hid_own, "section", FAR)
-    near_own = lax.ppermute(hid_own, "section", NEAR)
     hid_other = hidden_grad(weight_other, pre_other)
     far_other = lax.ppermute(hid_other, "section", FAR)
-    near_other = lax.ppermute(hid_other, "section", NEAR)
+    near = lax.ppermute(jnp.concatenate([hid_other, hid_own]), "section", NEAR)
     relay_own = lax.ppermute(far_own, "section", NEAR)
     relay_other = lax.ppermute(far_other, "section", NEAR)
 
@@ -159,7 +159,7 @@
         return out.astype(jnp.bfloat16)
 
     mine = back([hid_own, hid_other, far_own, far_other])
-    theirs = back([near_other, near_own, relay_other, relay_own])
+    theirs = back([near, relay_other, relay_own])
     back_rows = jnp.stack([mine, theirs], axis=1)
     returned = lax.all_to_all(
         back_rows, ("expert", "dp"), split_axis=0, concat_axis=0, tiled=True
@@ -170,8 +170,9 @@
     places = flat_ids * capacity + jnp.where(ranks == served, 0, 1)
     wanted = places[:, None] == jnp.arange(experts * capacity, dtype=jnp.int32)
     wanted = (wanted[:tokens] | wanted[tokens:]).astype(jnp.bfloat16)
+    own_cols = lax.dynamic_slice_in_dim(upstream, section * col_part, col_part, 1)
+    wanted, own_cols = lax.optimization_barrier((wanted, own_cols))
     total = jnp.dot(wanted, returned, preferred_element_type=jnp.float32)
-    own_cols = lax.dynamic_slice_in_dim(upstream, section * col_part, col_part, 1)
     return (own_cols.astype(jnp.float32) + total).astype(jnp.bfloat16)
 
 

time: 145 us -> 144 us (level)
    ppermute x1, waiting for transfers between devices: 4.2 us -> 6.92 us  [body(): far_other = lax.ppermute(hid_other, 'section', FAR)]
    ppermute x2 -> x1, starting transfers between devices: 5.28 us -> 3.14 us  [body(): near = lax.ppermute(jnp.concatenate([hid_other, hid_own]), 'section', NEAR)]
    unnamed x17 -> x9, local copies, waits for them, and re-layouts: 3.34 us -> 1.37 us
  transfers between devices with their start and end apart: 10 -> 9, of which waited for: 7 -> 7; matrix products, arithmetic and copies ran while one was open for 1% -> 2% of each run, Pallas kernels for 2% -> 2%
where the time goes in v4:
time: 144 us
  waiting for transfers between devices  69.6 us (48%)
  starting transfers between devices  63 us (44%)
  local copies, waits for them, and re-layouts  3.83 us (3%)
  Pallas kernels  3.26 us (2%)
  matrix products  3.22 us (2%)
    all_to_all x1, waiting for transfers between devices, body(): lax.all_to_all(rows, ('section', 'expert', 'dp'), split_axis=0, concat_ax...  29.9 us
    all_to_all x1, starting transfers between devices, body(): lax.all_to_all(rows, ('section', 'expert', 'dp'), split_axis=0, concat_ax...  28.8 us
    all_to_all x1, waiting for transfers between devices, body(): lax.all_to_all(back_rows, ('expert', 'dp'), split_axis=0, concat_axis=0,...  23.9 us
    all_to_all x1, starting transfers between devices, body(): lax.all_to_all(back_rows, ('expert', 'dp'), split_axis=0, concat_axis=0,...  10.5 us
    ppermute x1, waiting for transfers between devices, body(): far_other = lax.ppermute(hid_other, 'section', FAR)  6.92 us
    ppermute x1, starting transfers between devices, body(): far_other = lax.ppermute(hid_other, 'section', FAR)  6.23 us
    ppermute x1, starting transfers between devices, body(): weight_other = held(lax.ppermute(weight_own, 'section', NEAR), HELD_FLOPS)  4.14 us
    ppermute x1, waiting for transfers between devices, body(): relay_other = lax.ppermute(far_other, 'section', NEAR)  3.86 us
  transfers between devices with their start and end apart: 9, of which 7 were waited for; matrix products, arithmetic and copies ran while one was open for 2% of the time, Pallas kernels for 2%

profile of v4, /device:TPU:1, one launch (start us, length us, event | category | flops | bytes accessed | tf_op | source)
XLA Modules:
  0.0 143.6 jit_solution(17121526808080810584)
XLA Ops:
  0.0 4.1 %collective-permute-start = (bf16[352,2048]{1,0:T(8,128)(2,1)}, bf16[352,2048]{1,0:T(8,128)(2,1)S(1)}, u32[]{:S(2)}, u32[]{:S(2)}) collective-permute-start(bf16[352,2048]{1,0:T(8,128)(2,1)} %bitcast.53), channel_id=1, source_target_pairs={{0,256},{256,0},{512,768},{768,512},{1,257},{257,1},{513,769},{769... | collective-permute-start | bytes 4325384 | tf_op jit(solution)/shard_map/ppermute | solution.py:134
  4.2 2.8 %gated_rows.1 = bf16[256,2,1024]{2,1,0:T(2,128)(2,1)} custom-call(s32[1]{0:T(128)} %bitcast.3.kind_ref, f32[64]{0:T(128)} %table_ref.1, s32[2,128]{1,0:T(2,128)} %bitcast.50, s32[2,128]{1,0:T(2,128)} %bitcast.52, bf16[128,2048]{1,0:T(8,128)(2,1)} %up_ref.1), custom_call_target="tpu_custom_call" | custom-call | tf_op jit(solution)/shard_map/gated_rows/pallas_call | solution.py:68
  7.0 28.8 %all-to-all-start = ((bf16[256,2,1024]{2,1,0:T(2,128)(2,1)}), bf16[256,2,1024]{2,1,0:T(2,128)(2,1)S(1)}, u32[]{:S(2)}, u32[]{:S(2)}) async-start(bf16[256,2,1024]{2,1,0:T(2,128)(2,1)} %gated_rows.1), calls=%async_computation | async-start | bytes 2097152 | tf_op jit(solution)/shard_map/all_to_all | solution.py:124
  35.8 3.3 %collective-permute-start.1 = (bf16[352,256]{1,0:T(8,128)(2,1)S(1)}, bf16[352,256]{1,0:T(8,128)(2,1)S(1)}, u32[]{:S(2)}, u32[]{:S(2)}) collective-permute-start(bf16[352,256]{1,0:T(8,128)(2,1)S(1)} %select_bitcast_fusion), channel_id=1, source_target_pairs={{0,256},{256,0},{512,768},{768,512},{1,257},{257,1},{513,769},{769... | collective-permute-start | bytes 540680 | tf_op jit(solution)/shard_map/ppermute | solution.py:137
  39.2 29.9 %all-to-all-done = bf16[256,2,1024]{2,1,0:T(2,128)(2,1)S(1)} async-done(((bf16[256,2,1024]{2,1,0:T(2,128)(2,1)}), bf16[256,2,1024]{2,1,0:T(2,128)(2,1)S(1)}, u32[]{:S(2)}, u32[]{:S(2)}) %all-to-all-start) | async-done | bytes 1048608 | tf_op jit(solution)/shard_map/all_to_all | solution.py:124
  69.4 1.1 copy-done.3
  70.5 0.6 fusion.2.after_ref
  71.1 0.6 fusion.3
  71.6 6.2 %collective-permute-start.3 = (bf16[352,256]{1,0:T(8,128)(2,1)S(1)}, bf16[352,256]{1,0:T(8,128)(2,1)S(1)}, u32[]{:S(2)}, u32[]{:S(2)}) collective-permute-start(bf16[352,256]{1,0:T(8,128)(2,1)S(1)} %fusion.3), channel_id=1, source_target_pairs={{0,512},{512,0},{256,768},{768,256},{1,513},{513,1},{257,769},{769... | collective-permute-start | bytes 540680 | tf_op jit(solution)/shard_map/ppermute | solution.py:148
  77.9 1.9 %collective-permute-start.2 = (bf16[352,256]{1,0:T(8,128)(2,1)S(1)}, bf16[352,256]{1,0:T(8,128)(2,1)S(1)}, u32[]{:S(2)}, u32[]{:S(2)}) collective-permute-start(bf16[352,256]{1,0:T(8,128)(2,1)S(1)} %fusion.2.after_ref), channel_id=1, source_target_pairs={{0,512},{512,0},{256,768},{768,256},{1,513},{513,1},{257,769},{769... | collective-permute-start | bytes 540680 | tf_op jit(solution)/shard_map/ppermute | solution.py:146
  79.8 3.1 %collective-permute-start.4 = (bf16[704,256]{1,0:T(8,128)(2,1)S(1)}, bf16[704,256]{1,0:T(8,128)(2,1)S(1)}, u32[]{:S(2)}, u32[]{:S(2)}) collective-permute-start(bf16[704,256]{1,0:T(8,128)(2,1)S(1)} %pad_maximum_fusion.1), channel_id=1, source_target_pairs={{0,256},{256,0},{512,768},{768,512},{1,257},{257,1},{513,769},{769... | collective-permute-start | bytes 1081352 | tf_op jit(solution)/shard_map/ppermute | solution.py:149
  83.5 6.9 %collective-permute-done.3 = bf16[352,256]{1,0:T(8,128)(2,1)S(1)} collective-permute-done((bf16[352,256]{1,0:T(8,128)(2,1)S(1)}, bf16[352,256]{1,0:T(8,128)(2,1)S(1)}, u32[]{:S(2)}, u32[]{:S(2)}) %collective-permute-start.3) | collective-permute-done | bytes 180256 | tf_op jit(solution)/shard_map/ppermute | solution.py:148
  90.4 1.9 %collective-permute-start.5 = (bf16[352,256]{1,0:T(8,128)(2,1)S(1)}, bf16[352,256]{1,0:T(8,128)(2,1)S(1)}, u32[]{:S(2)}, u32[]{:S(2)}) collective-permute-start(bf16[352,256]{1,0:T(8,128)(2,1)S(1)} %collective-permute-done.3), channel_id=1, source_target_pairs={{0,256},{256,0},{512,768},{768,512},{1,257},{257,1},{513,769},{769... | collective-permute-start | bytes 540680 | tf_op jit(solution)/shard_map/ppermute | solution.py:151
  92.6 3.0 %collective-permute-start.6 = (bf16[352,256]{1,0:T(8,128)(2,1)S(1)}, bf16[352,256]{1,0:T(8,128)(2,1)S(1)}, u32[]{:S(2)}, u32[]{:S(2)}) collective-permute-start(bf16[352,256]{1,0:T(8,128)(2,1)S(1)} %collective-permute-done.2), channel_id=1, source_target_pairs={{0,256},{256,0},{512,768},{768,512},{1,257},{257,1},{513,769},{769... | collective-permute-start | bytes 540680 | tf_op jit(solution)/shard_map/ppermute | solution.py:150
  95.7 0.6 fusion.4
  96.3 2.3 %collective-permute-done.4 = bf16[704,256]{1,0:T(8,128)(2,1)S(1)} collective-permute-done((bf16[704,256]{1,0:T(8,128)(2,1)S(1)}, bf16[704,256]{1,0:T(8,128)(2,1)S(1)}, u32[]{:S(2)}, u32[]{:S(2)}) %collective-permute-start.4) | collective-permute-done | bytes 360480 | tf_op jit(solution)/shard_map/ppermute | solution.py:149
  98.6 3.9 %collective-permute-done.5 = bf16[352,256]{1,0:T(8,128)(2,1)S(1)} collective-permute-done((bf16[352,256]{1,0:T(8,128)(2,1)S(1)}, bf16[352,256]{1,0:T(8,128)(2,1)S(1)}, u32[]{:S(2)}, u32[]{:S(2)}) %collective-permute-start.5) | collective-permute-done | bytes 180256 | tf_op jit(solution)/shard_map/ppermute | solution.py:151
  102.5 2.3 %collective-permute-done.6 = bf16[352,256]{1,0:T(8,128)(2,1)S(1)} collective-permute-done((bf16[352,256]{1,0:T(8,128)(2,1)S(1)}, bf16[352,256]{1,0:T(8,128)(2,1)S(1)}, u32[]{:S(2)}, u32[]{:S(2)}) %collective-permute-start.6) | collective-permute-done | bytes 180256 | tf_op jit(solution)/shard_map/ppermute | solution.py:150
  104.8 0.6 fusion.5
  105.5 1.3 copy.11
  106.8 10.5 %all-to-all-start.1 = ((bf16[256,2,512]{2,1,0:T(2,128)(2,1)}), bf16[256,2,512]{2,1,0:T(2,128)(2,1)S(1)}, u32[]{:S(2)}, u32[]{:S(2)}) async-start(bf16[256,2,512]{2,1,0:T(2,128)(2,1)} %copy.11), calls=%async_computation.1 | async-start | bytes 1048576 | tf_op jit(solution)/shard_map/all_to_all | solution.py:164
  117.3 0.9 constant_dynamic-slice_fusion
  118.6 23.9 %all-to-all-done.1 = bf16[256,2,512]{2,1,0:T(2,128)(2,1)S(1)} async-done(((bf16[256,2,512]{2,1,0:T(2,128)(2,1)}), bf16[256,2,512]{2,1,0:T(2,128)(2,1)S(1)}, u32[]{:S(2)}, u32[]{:S(2)}) %all-to-all-start.1) | async-done | bytes 524320 | tf_op jit(solution)/shard_map/all_to_all | solution.py:164
  142.7 0.9 fusion.6
  (22 shorter events, 1.7 us)
Async XLA Ops:
  0.0 39.2 %collective-permute-start = (bf16[352,2048]{1,0:T(8,128)(2,1)}, bf16[352,2048]{1,0:T(8,128)(2,1)S(1)}, u32[]{:S(2)}, u32[]{:S(2)}) collective-permute-start(bf16[352,2048]{1,0:T(8,128)(2,1)} %bitcast.53), channel_id=1, source_target_pairs={{0,256},{256,0},{512,768},{768,512},{1,257},{257,1},{513,769},{769... | collective-permute-start | bytes 4325384 | tf_op jit(solution)/shard_map/ppermute | solution.py:134
  7.0 28.8 %copy-start.1 = (bf16[1,256,2,352]{1,3,2,0:T(8,128)(2,1)S(1)}, bf16[1,256,2,352]{1,3,2,0:T(8,128)(2,1)}, u32[]{:S(2)}) copy-start(bf16[1,256,2,352]{1,3,2,0:T(8,128)(2,1)} %param.13) | copy-start | bytes 1081348
  7.0 62.1 %all-to-all-start = ((bf16[256,2,1024]{2,1,0:T(2,128)(2,1)}), bf16[256,2,1024]{2,1,0:T(2,128)(2,1)S(1)}, u32[]{:S(2)}, u32[]{:S(2)}) async-start(bf16[256,2,1024]{2,1,0:T(2,128)(2,1)} %gated_rows.1), calls=%async_computation | async-start | bytes 2097152 | tf_op jit(solution)/shard_map/all_to_all | solution.py:124
  35.8 35.2 %collective-permute-start.1 = (bf16[352,256]{1,0:T(8,128)(2,1)S(1)}, bf16[352,256]{1,0:T(8,128)(2,1)S(1)}, u32[]{:S(2)}, u32[]{:S(2)}) collective-permute-start(bf16[352,256]{1,0:T(8,128)(2,1)S(1)} %select_bitcast_fusion), channel_id=1, source_target_pairs={{0,256},{256,0},{512,768},{768,512},{1,257},{257,1},{513,769},{769... | collective-permute-start | bytes 540680 | tf_op jit(solution)/shard_map/ppermute | solution.py:137
  69.1 1.4 copy-start.3
  71.1 11.9 %copy-start = (bf16[1,512,1408]{2,1,0:T(8,128)(2,1)S(1)}, bf16[1,512,1408]{2,1,0:T(8,128)(2,1)}, u32[]{:S(2)}) copy-start(bf16[1,512,1408]{2,1,0:T(8,128)(2,1)} %param.11) | copy-start | bytes 4325380
  71.6 18.7 %collective-permute-start.3 = (bf16[352,256]{1,0:T(8,128)(2,1)S(1)}, bf16[352,256]{1,0:T(8,128)(2,1)S(1)}, u32[]{:S(2)}, u32[]{:S(2)}) collective-permute-start(bf16[352,256]{1,0:T(8,128)(2,1)S(1)} %fusion.3), channel_id=1, source_target_pairs={{0,512},{512,0},{256,768},{768,256},{1,513},{513,1},{257,769},{769... | collective-permute-start | bytes 540680 | tf_op jit(solution)/shard_map/ppermute | solution.py:148
  77.9 14.7 %collective-permute-start.2 = (bf16[352,256]{1,0:T(8,128)(2,1)S(1)}, bf16[352,256]{1,0:T(8,128)(2,1)S(1)}, u32[]{:S(2)}, u32[]{:S(2)}) collective-permute-start(bf16[352,256]{1,0:T(8,128)(2,1)S(1)} %fusion.2.after_ref), channel_id=1, source_target_pairs={{0,512},{512,0},{256,768},{768,256},{1,513},{513,1},{257,769},{769... | collective-permute-start | bytes 540680 | tf_op jit(solution)/shard_map/ppermute | solution.py:146
  79.8 18.7 %collective-permute-start.4 = (bf16[704,256]{1,0:T(8,128)(2,1)S(1)}, bf16[704,256]{1,0:T(8,128)(2,1)S(1)}, u32[]{:S(2)}, u32[]{:S(2)}) collective-permute-start(bf16[704,256]{1,0:T(8,128)(2,1)S(1)} %pad_maximum_fusion.1), channel_id=1, source_target_pairs={{0,256},{256,0},{512,768},{768,512},{1,257},{257,1},{513,769},{769... | collective-permute-start | bytes 1081352 | tf_op jit(solution)/shard_map/ppermute | solution.py:149
  90.4 12.1 %collective-permute-start.5 = (bf16[352,256]{1,0:T(8,128)(2,1)S(1)}, bf16[352,256]{1,0:T(8,128)(2,1)S(1)}, u32[]{:S(2)}, u32[]{:S(2)}) collective-permute-start(bf16[352,256]{1,0:T(8,128)(2,1)S(1)} %collective-permute-done.3), channel_id=1, source_target_pairs={{0,256},{256,0},{512,768},{768,512},{1,257},{257,1},{513,769},{769... | collective-permute-start | bytes 540680 | tf_op jit(solution)/shard_map/ppermute | solution.py:151
  92.6 12.2 %collective-permute-start.6 = (bf16[352,256]{1,0:T(8,128)(2,1)S(1)}, bf16[352,256]{1,0:T(8,128)(2,1)S(1)}, u32[]{:S(2)}, u32[]{:S(2)}) collective-permute-start(bf16[352,256]{1,0:T(8,128)(2,1)S(1)} %collective-permute-done.2), channel_id=1, source_target_pairs={{0,256},{256,0},{512,768},{768,512},{1,257},{257,1},{513,769},{769... | collective-permute-start | bytes 540680 | tf_op jit(solution)/shard_map/ppermute | solution.py:150
  105.5 12.8 %copy-start.2 = (s32[128,2]{0,1:T(2,128)S(1)}, s32[128,2]{0,1:T(2,128)}, u32[]{:S(2)}) copy-start(s32[128,2]{0,1:T(2,128)} %param.8) | copy-start | bytes 3076
  106.8 35.7 %all-to-all-start.1 = ((bf16[256,2,512]{2,1,0:T(2,128)(2,1)}), bf16[256,2,512]{2,1,0:T(2,128)(2,1)S(1)}, u32[]{:S(2)}, u32[]{:S(2)}) async-start(bf16[256,2,512]{2,1,0:T(2,128)(2,1)} %copy.11), calls=%async_computation.1 | async-start | bytes 1048576 | tf_op jit(solution)/shard_map/all_to_all | solution.py:164

commit v5 on v4

--- a/solution.py
+++ b/solution.py
@@ -7,6 +7,7 @@
 
 NEAR = [(0, 1), (1, 0), (2, 3), (3, 2)]
 FAR = [(0, 2), (2, 0), (1, 3), (3, 1)]
+DIAGONAL = [(0, 3), (3, 0), (1, 2), (2, 1)]
 HELD_FLOPS = 100_000_000_000
 ROWS_VMEM = 65_200_000
 
@@ -142,12 +143,13 @@
         sig = jax.nn.sigmoid(pre_act)
         return (proj * (sig * (1.0 + pre_act * (1.0 - sig)))).astype(jnp.bfloat16)
 
+    hid_other = hidden_grad(weight_other, pre_other)
+    far_other = lax.ppermute(hid_other, "section", FAR)
+    weight_own, hid_other = lax.optimization_barrier((weight_own, hid_other))
     hid_own = hidden_grad(weight_own, pre_mine)
     far_own = lax.ppermute(hid_own, "section", FAR)
-    hid_other = hidden_grad(weight_other, pre_other)
-    far_other = lax.ppermute(hid_other, "section", FAR)
     near = lax.ppermute(jnp.concatenate([hid_other, hid_own]), "section", NEAR)
-    relay_own = lax.ppermute(far_own, "section", NEAR)
+    diagonal_own = lax.ppermute(hid_own, "section", DIAGONAL)
     relay_other = lax.ppermute(far_other, "section", NEAR)
 
     parts = reorder(section, w_up[0], hid_own)
@@ -159,7 +161,7 @@
         return out.astype(jnp.bfloat16)
 
     mine = back([hid_own, hid_other, far_own, far_other])
-    theirs = back([near, relay_other, relay_own])
+    theirs = back([near, relay_other, diagonal_own])
     back_rows = jnp.stack([mine, theirs], axis=1)
     returned = lax.all_to_all(
         back_rows, ("expert", "dp"), split_axis=0, concat_axis=0, tiled=True

time: 144 us -> 145 us (level)
  starting transfers between devices: 63 us -> 65.8 us
    ppermute x1, waiting for transfers between devices: 6.92 us -> 2.09 us  [body(): far_other = lax.ppermute(hid_other, 'section', FAR)]
    ppermute x1, waiting for transfers between devices: 0.32 us -> 4.92 us  [body(): far_own = lax.ppermute(hid_own, 'section', FAR)]
    ppermute x1, waiting for transfers between devices: 2.33 us -> 4.61 us  [body(): near = lax.ppermute(jnp.concatenate([hid_other, hid_own]), 'section', NEAR)]
    ppermute x1, waiting for transfers between devices: 2.34 us -> 0.65 us  [body(): diagonal_own = lax.ppermute(hid_own, 'section', DIAGONAL)]
    all_to_all x1, starting transfers between devices: 10.5 us -> 12.2 us  [body(): lax.all_to_all(back_rows, ('expert', 'dp'), split_axis=0, concat_axis=0,...]
    ppermute x1, waiting for transfers between devices: 3.86 us -> 2.33 us  [body(): relay_other = lax.ppermute(far_other, 'section', NEAR)]
where the time goes in v5:
time: 145 us; the launch traced here: 144 us
  waiting for transfers between devices  68.4 us (47%)
  starting transfers between devices  65.8 us (45%)
  Pallas kernels  3.26 us (2%)
  matrix products  3.22 us (2%)
  local copies, waits for them, and re-layouts  2.75 us (2%)
    all_to_all x1, waiting for transfers between devices, body(): lax.all_to_all(rows, ('section', 'expert', 'dp'), split_axis=0, concat_ax...  29.9 us
    all_to_all x1, starting transfers between devices, body(): lax.all_to_all(rows, ('section', 'expert', 'dp'), split_axis=0, concat_ax...  28.8 us
    all_to_all x1, waiting for transfers between devices, body(): lax.all_to_all(back_rows, ('expert', 'dp'), split_axis=0, concat_axis=0,...  23.8 us
    all_to_all x1, starting transfers between devices, body(): lax.all_to_all(back_rows, ('expert', 'dp'), split_axis=0, concat_axis=0,...  12.2 us
    ppermute x1, starting transfers between devices, body(): far_other = lax.ppermute(hid_other, 'section', FAR)  6.23 us
    ppermute x1, waiting for transfers between devices, body(): far_own = lax.ppermute(hid_own, 'section', FAR)  4.92 us
    ppermute x1, waiting for transfers between devices, body(): near = lax.ppermute(jnp.concatenate([hid_other, hid_own]), 'section', NEAR)  4.61 us
    ppermute x1, starting transfers between devices, body(): diagonal_own = lax.ppermute(hid_own, 'section', DIAGONAL)  4.21 us
  transfers between devices with their start and end apart: 9, of which 7 were waited for; matrix products, arithmetic and copies ran while one was open for 2% of the time, Pallas kernels for 2%

profile of v5, /device:TPU:1, one launch (start us, length us, event | category | flops | bytes accessed | tf_op | source)
XLA Modules:
  0.0 144.2 jit_solution(6939947153818667496)
XLA Ops:
  0.0 4.1 %collective-permute-start = (bf16[352,2048]{1,0:T(8,128)(2,1)}, bf16[352,2048]{1,0:T(8,128)(2,1)S(1)}, u32[]{:S(2)}, u32[]{:S(2)}) collective-permute-start(bf16[352,2048]{1,0:T(8,128)(2,1)} %bitcast.46), channel_id=1, source_target_pairs={{0,256},{256,0},{512,768},{768,512},{1,257},{257,1},{513,769},{769... | collective-permute-start | bytes 4325384 | tf_op jit(solution)/shard_map/ppermute | solution.py:135
  4.2 2.8 %gated_rows.1 = bf16[256,2,1024]{2,1,0:T(2,128)(2,1)} custom-call(s32[1]{0:T(128)} %bitcast.4.kind_ref, f32[64]{0:T(128)} %table_ref.1, s32[2,128]{1,0:T(2,128)} %bitcast.43, s32[2,128]{1,0:T(2,128)} %bitcast.45, bf16[128,2048]{1,0:T(8,128)(2,1)} %up_ref.1), custom_call_target="tpu_custom_call" | custom-call | tf_op jit(solution)/shard_map/gated_rows/pallas_call | solution.py:69
  7.0 28.8 %all-to-all-start = ((bf16[256,2,1024]{2,1,0:T(2,128)(2,1)}), bf16[256,2,1024]{2,1,0:T(2,128)(2,1)S(1)}, u32[]{:S(2)}, u32[]{:S(2)}) async-start(bf16[256,2,1024]{2,1,0:T(2,128)(2,1)} %gated_rows.1), calls=%async_computation | async-start | bytes 2097152 | tf_op jit(solution)/shard_map/all_to_all | solution.py:125
  35.8 3.3 %collective-permute-start.1 = (bf16[352,256]{1,0:T(8,128)(2,1)S(1)}, bf16[352,256]{1,0:T(8,128)(2,1)S(1)}, u32[]{:S(2)}, u32[]{:S(2)}) collective-permute-start(bf16[352,256]{1,0:T(8,128)(2,1)S(1)} %select_bitcast_fusion), channel_id=1, source_target_pairs={{0,256},{256,0},{512,768},{768,512},{1,257},{257,1},{513,769},{769... | collective-permute-start | bytes 540680 | tf_op jit(solution)/shard_map/ppermute | solution.py:138
  39.2 29.9 %all-to-all-done = bf16[256,2,1024]{2,1,0:T(2,128)(2,1)S(1)} async-done(((bf16[256,2,1024]{2,1,0:T(2,128)(2,1)}), bf16[256,2,1024]{2,1,0:T(2,128)(2,1)S(1)}, u32[]{:S(2)}, u32[]{:S(2)}) %all-to-all-start) | async-done | bytes 1048608 | tf_op jit(solution)/shard_map/all_to_all | solution.py:125
  69.4 0.6 fusion.1
  70.0 6.2 %collective-permute-start.3 = (bf16[352,256]{1,0:T(8,128)(2,1)S(1)}, bf16[352,256]{1,0:T(8,128)(2,1)S(1)}, u32[]{:S(2)}, u32[]{:S(2)}) collective-permute-start(bf16[352,256]{1,0:T(8,128)(2,1)S(1)} %fusion.1), channel_id=1, source_target_pairs={{0,512},{512,0},{256,768},{768,256},{1,513},{513,1},{257,769},{769... | collective-permute-start | bytes 540680 | tf_op jit(solution)/shard_map/ppermute | solution.py:147
  76.2 0.6 fusion.2.after_ref
  76.8 1.9 %collective-permute-start.2 = (bf16[352,256]{1,0:T(8,128)(2,1)S(1)}, bf16[352,256]{1,0:T(8,128)(2,1)S(1)}, u32[]{:S(2)}, u32[]{:S(2)}) collective-permute-start(bf16[352,256]{1,0:T(8,128)(2,1)S(1)} %fusion.2.after_ref), channel_id=1, source_target_pairs={{0,512},{512,0},{256,768},{768,256},{1,513},{513,1},{257,769},{769... | collective-permute-start | bytes 540680 | tf_op jit(solution)/shard_map/ppermute | solution.py:150
  78.8 3.1 %collective-permute-start.4 = (bf16[704,256]{1,0:T(8,128)(2,1)S(1)}, bf16[704,256]{1,0:T(8,128)(2,1)S(1)}, u32[]{:S(2)}, u32[]{:S(2)}) collective-permute-start(bf16[704,256]{1,0:T(8,128)(2,1)S(1)} %pad_maximum_fusion.1), channel_id=1, source_target_pairs={{0,256},{256,0},{512,768},{768,512},{1,257},{257,1},{513,769},{769... | collective-permute-start | bytes 1081352 | tf_op jit(solution)/shard_map/ppermute | solution.py:151
  81.9 4.2 %collective-permute-start.6 = (bf16[352,256]{1,0:T(8,128)(2,1)S(1)}, bf16[352,256]{1,0:T(8,128)(2,1)S(1)}, u32[]{:S(2)}, u32[]{:S(2)}) collective-permute-start(bf16[352,256]{1,0:T(8,128)(2,1)S(1)} %fusion.2.after_ref), channel_id=1, source_target_pairs={{0,768},{768,0},{256,512},{512,256},{1,769},{769,1},{257,513},{513... | collective-permute-start | bytes 540680 | tf_op jit(solution)/shard_map/ppermute | solution.py:152
  86.6 2.1 %collective-permute-done.3 = bf16[352,256]{1,0:T(8,128)(2,1)S(1)} collective-permute-done((bf16[352,256]{1,0:T(8,128)(2,1)S(1)}, bf16[352,256]{1,0:T(8,128)(2,1)S(1)}, u32[]{:S(2)}, u32[]{:S(2)}) %collective-permute-start.3) | collective-permute-done | bytes 180256 | tf_op jit(solution)/shard_map/ppermute | solution.py:147
  88.7 1.9 %collective-permute-start.5 = (bf16[352,256]{1,0:T(8,128)(2,1)S(1)}, bf16[352,256]{1,0:T(8,128)(2,1)S(1)}, u32[]{:S(2)}, u32[]{:S(2)}) collective-permute-start(bf16[352,256]{1,0:T(8,128)(2,1)S(1)} %collective-permute-done.3), channel_id=1, source_target_pairs={{0,256},{256,0},{512,768},{768,512},{1,257},{257,1},{513,769},{769... | collective-permute-start | bytes 540680 | tf_op jit(solution)/shard_map/ppermute | solution.py:153
  90.6 4.9 %collective-permute-done.2 = bf16[352,256]{1,0:T(8,128)(2,1)S(1)} collective-permute-done((bf16[352,256]{1,0:T(8,128)(2,1)S(1)}, bf16[352,256]{1,0:T(8,128)(2,1)S(1)}, u32[]{:S(2)}, u32[]{:S(2)}) %collective-permute-start.2) | collective-permute-done | bytes 180256 | tf_op jit(solution)/shard_map/ppermute | solution.py:150
  95.5 0.6 fusion.3
  96.1 0.7 collective-permute-done.6
  96.8 4.6 %collective-permute-done.4 = bf16[704,256]{1,0:T(8,128)(2,1)S(1)} collective-permute-done((bf16[704,256]{1,0:T(8,128)(2,1)S(1)}, bf16[704,256]{1,0:T(8,128)(2,1)S(1)}, u32[]{:S(2)}, u32[]{:S(2)}) %collective-permute-start.4) | collective-permute-done | bytes 360480 | tf_op jit(solution)/shard_map/ppermute | solution.py:151
  101.4 2.3 %collective-permute-done.5 = bf16[352,256]{1,0:T(8,128)(2,1)S(1)} collective-permute-done((bf16[352,256]{1,0:T(8,128)(2,1)S(1)}, bf16[352,256]{1,0:T(8,128)(2,1)S(1)}, u32[]{:S(2)}, u32[]{:S(2)}) %collective-permute-start.5) | collective-permute-done | bytes 180256 | tf_op jit(solution)/shard_map/ppermute | solution.py:153
  103.7 0.6 fusion.4
  104.4 1.3 copy.11
  105.7 12.2 %all-to-all-start.1 = ((bf16[256,2,512]{2,1,0:T(2,128)(2,1)}), bf16[256,2,512]{2,1,0:T(2,128)(2,1)S(1)}, u32[]{:S(2)}, u32[]{:S(2)}) async-start(bf16[256,2,512]{2,1,0:T(2,128)(2,1)} %copy.11), calls=%async_computation.1 | async-start | bytes 1048576 | tf_op jit(solution)/shard_map/all_to_all | solution.py:166
  117.9 0.9 constant_dynamic-slice_fusion
  119.2 23.8 %all-to-all-done.1 = bf16[256,2,512]{2,1,0:T(2,128)(2,1)S(1)} async-done(((bf16[256,2,512]{2,1,0:T(2,128)(2,1)}), bf16[256,2,512]{2,1,0:T(2,128)(2,1)S(1)}, u32[]{:S(2)}, u32[]{:S(2)}) %all-to-all-start.1) | async-done | bytes 524320 | tf_op jit(solution)/shard_map/all_to_all | solution.py:166
  143.3 0.9 fusion.5
  (22 shorter events, 1.4 us)
Async XLA Ops:
  0.0 39.2 %collective-permute-start = (bf16[352,2048]{1,0:T(8,128)(2,1)}, bf16[352,2048]{1,0:T(8,128)(2,1)S(1)}, u32[]{:S(2)}, u32[]{:S(2)}) collective-permute-start(bf16[352,2048]{1,0:T(8,128)(2,1)} %bitcast.46), channel_id=1, source_target_pairs={{0,256},{256,0},{512,768},{768,512},{1,257},{257,1},{513,769},{769... | collective-permute-start | bytes 4325384 | tf_op jit(solution)/shard_map/ppermute | solution.py:135
  7.0 28.8 %copy-start.1 = (bf16[1,256,2,352]{1,3,2,0:T(8,128)(2,1)S(1)}, bf16[1,256,2,352]{1,3,2,0:T(8,128)(2,1)}, u32[]{:S(2)}) copy-start(bf16[1,256,2,352]{1,3,2,0:T(8,128)(2,1)} %param.13) | copy-start | bytes 1081348
  7.0 62.1 %all-to-all-start = ((bf16[256,2,1024]{2,1,0:T(2,128)(2,1)}), bf16[256,2,1024]{2,1,0:T(2,128)(2,1)S(1)}, u32[]{:S(2)}, u32[]{:S(2)}) async-start(bf16[256,2,1024]{2,1,0:T(2,128)(2,1)} %gated_rows.1), calls=%async_computation | async-start | bytes 2097152 | tf_op jit(solution)/shard_map/all_to_all | solution.py:125
  35.8 33.5 %collective-permute-start.1 = (bf16[352,256]{1,0:T(8,128)(2,1)S(1)}, bf16[352,256]{1,0:T(8,128)(2,1)S(1)}, u32[]{:S(2)}, u32[]{:S(2)}) collective-permute-start(bf16[352,256]{1,0:T(8,128)(2,1)S(1)} %select_bitcast_fusion), channel_id=1, source_target_pairs={{0,256},{256,0},{512,768},{768,512},{1,257},{257,1},{513,769},{769... | collective-permute-start | bytes 540680 | tf_op jit(solution)/shard_map/ppermute | solution.py:138
  69.4 6.8 %copy-start.3 = (bf16[1,352,2048]{2,1,0:T(8,128)(2,1)S(1)}, bf16[1,352,2048]{2,1,0:T(8,128)(2,1)}, u32[]{:S(2)}) copy-start(bf16[1,352,2048]{2,1,0:T(8,128)(2,1)} %param.12) | copy-start | bytes 4325380
  70.0 18.7 %collective-permute-start.3 = (bf16[352,256]{1,0:T(8,128)(2,1)S(1)}, bf16[352,256]{1,0:T(8,128)(2,1)S(1)}, u32[]{:S(2)}, u32[]{:S(2)}) collective-permute-start(bf16[352,256]{1,0:T(8,128)(2,1)S(1)} %fusion.1), channel_id=1, source_target_pairs={{0,512},{512,0},{256,768},{768,256},{1,513},{513,1},{257,769},{769... | collective-permute-start | bytes 540680 | tf_op jit(solution)/shard_map/ppermute | solution.py:147
  76.2 9.9 %copy-start = (bf16[1,512,1408]{2,1,0:T(8,128)(2,1)S(1)}, bf16[1,512,1408]{2,1,0:T(8,128)(2,1)}, u32[]{:S(2)}) copy-start(bf16[1,512,1408]{2,1,0:T(8,128)(2,1)} %param.11) | copy-start | bytes 4325380
  76.8 18.7 %collective-permute-start.2 = (bf16[352,256]{1,0:T(8,128)(2,1)S(1)}, bf16[352,256]{1,0:T(8,128)(2,1)S(1)}, u32[]{:S(2)}, u32[]{:S(2)}) collective-permute-start(bf16[352,256]{1,0:T(8,128)(2,1)S(1)} %fusion.2.after_ref), channel_id=1, source_target_pairs={{0,512},{512,0},{256,768},{768,256},{1,513},{513,1},{257,769},{769... | collective-permute-start | bytes 540680 | tf_op jit(solution)/shard_map/ppermute | solution.py:150
  78.8 22.6 %collective-permute-start.4 = (bf16[704,256]{1,0:T(8,128)(2,1)S(1)}, bf16[704,256]{1,0:T(8,128)(2,1)S(1)}, u32[]{:S(2)}, u32[]{:S(2)}) collective-permute-start(bf16[704,256]{1,0:T(8,128)(2,1)S(1)} %pad_maximum_fusion.1), channel_id=1, source_target_pairs={{0,256},{256,0},{512,768},{768,512},{1,257},{257,1},{513,769},{769... | collective-permute-start | bytes 1081352 | tf_op jit(solution)/shard_map/ppermute | solution.py:151
  81.9 14.8 %collective-permute-start.6 = (bf16[352,256]{1,0:T(8,128)(2,1)S(1)}, bf16[352,256]{1,0:T(8,128)(2,1)S(1)}, u32[]{:S(2)}, u32[]{:S(2)}) collective-permute-start(bf16[352,256]{1,0:T(8,128)(2,1)S(1)} %fusion.2.after_ref), channel_id=1, source_target_pairs={{0,768},{768,0},{256,512},{512,256},{1,769},{769,1},{257,513},{513... | collective-permute-start | bytes 540680 | tf_op jit(solution)/shard_map/ppermute | solution.py:152
  88.7 15.0 %collective-permute-start.5 = (bf16[352,256]{1,0:T(8,128)(2,1)S(1)}, bf16[352,256]{1,0:T(8,128)(2,1)S(1)}, u32[]{:S(2)}, u32[]{:S(2)}) collective-permute-start(bf16[352,256]{1,0:T(8,128)(2,1)S(1)} %collective-permute-done.3), channel_id=1, source_target_pairs={{0,256},{256,0},{512,768},{768,512},{1,257},{257,1},{513,769},{769... | collective-permute-start | bytes 540680 | tf_op jit(solution)/shard_map/ppermute | solution.py:153
  104.4 14.5 %copy-start.2 = (s32[128,2]{0,1:T(2,128)S(1)}, s32[128,2]{0,1:T(2,128)}, u32[]{:S(2)}) copy-start(s32[128,2]{0,1:T(2,128)} %param.8) | copy-start | bytes 3076
  105.7 37.3 %all-to-all-start.1 = ((bf16[256,2,512]{2,1,0:T(2,128)(2,1)}), bf16[256,2,512]{2,1,0:T(2,128)(2,1)S(1)}, u32[]{:S(2)}, u32[]{:S(2)}) async-start(bf16[256,2,512]{2,1,0:T(2,128)(2,1)} %copy.11), calls=%async_computation.1 | async-start | bytes 1048576 | tf_op jit(solution)/shard_map/all_to_all | solution.py:166

commit v6 on v4

--- a/solution.py
+++ b/solution.py
@@ -7,6 +7,7 @@
 
 NEAR = [(0, 1), (1, 0), (2, 3), (3, 2)]
 FAR = [(0, 2), (2, 0), (1, 3), (3, 1)]
+DIAGONAL = [(0, 3), (3, 0), (1, 2), (2, 1)]
 HELD_FLOPS = 100_000_000_000
 ROWS_VMEM = 65_200_000
 
@@ -75,6 +76,33 @@
     )(kind.reshape(1), table, ids, index, upstream)
 
 
+def join_kernel(mine_ref, near_ref, diagonal_ref, relay_ref, w_ref, out_ref):
+    total, at = None, 0
+    for piece in (near_ref, diagonal_ref, relay_ref):
+        depth = piece.shape[0]
+        term = lax.dot_general(
+            piece[...],
+            w_ref[at : at + depth],
+            (((0,), (0,)), ((), ())),
+            preferred_element_type=jnp.float32,
+        )
+        total, at = term if total is None else total + term, at + depth
+    out_ref[:, 0, :] = mine_ref[...]
+    out_ref[:, 1, :] = total.astype(out_ref.dtype)
+
+
+def join(mine, near, diagonal, relay, w):
+    vmem = pl.BlockSpec(memory_space=pltpu.VMEM)
+    return pl.pallas_call(
+        join_kernel,
+        out_shape=jax.ShapeDtypeStruct((mine.shape[0], 2, mine.shape[1]), mine.dtype),
+        in_specs=[vmem] * 5,
+        out_specs=vmem,
+        compiler_params=pltpu.CompilerParams(vmem_limit_bytes=8 << 20),
+        name="join",
+    )(mine, near, diagonal, relay, w)
+
+
 def reorder_kernel(section_ref, w_ref, after_ref, out_ref):
     del after_ref
     flipped = w_ref[...].T
@@ -144,11 +172,12 @@
 
     hid_own = hidden_grad(weight_own, pre_mine)
     far_own = lax.ppermute(hid_own, "section", FAR)
+    pre_other, weight_other, hid_own = lax.optimization_barrier((pre_other, weight_other, hid_own))
     hid_other = hidden_grad(weight_other, pre_other)
+    near = lax.ppermute(jnp.concatenate([hid_other, hid_own]), "section", NEAR)
     far_other = lax.ppermute(hid_other, "section", FAR)
-    near = lax.ppermute(jnp.concatenate([hid_other, hid_own]), "section", NEAR)
+    diagonal_other = lax.ppermute(hid_other, "section", DIAGONAL)
     relay_own = lax.ppermute(far_own, "section", NEAR)
-    relay_other = lax.ppermute(far_other, "section", NEAR)
 
     parts = reorder(section, w_up[0], hid_own)
 
@@ -159,8 +188,7 @@
         return out.astype(jnp.bfloat16)
 
     mine = back([hid_own, hid_other, far_own, far_other])
-    theirs = back([near, relay_other, relay_own])
-    back_rows = jnp.stack([mine, theirs], axis=1)
+    back_rows = join(mine, near, diagonal_other, relay_own, parts)
     returned = lax.all_to_all(
         back_rows, ("expert", "dp"), split_axis=0, concat_axis=0, tiled=True
     ).reshape(experts * capacity, col_part)

time: 144 us -> 144 us (level)
  Pallas kernels: 3.26 us -> 4.89 us
    ppermute x1, starting transfers between devices: 6.23 us -> 1.92 us  [body(): far_other = lax.ppermute(hid_other, 'section', FAR)]
    ppermute x1, starting transfers between devices: 1.92 us -> 6.23 us  [body(): far_own = lax.ppermute(hid_own, 'section', FAR)]
    ppermute x1, waiting for transfers between devices: 3.86 us -> 0.64 us  [body(): diagonal_other = lax.ppermute(hid_other, 'section', DIAGONAL)]
    ppermute x1, starting transfers between devices: 1.91 us -> 4.21 us  [body(): diagonal_other = lax.ppermute(hid_other, 'section', DIAGONAL)]
    ppermute x1, waiting for transfers between devices: 2.33 us -> 4.61 us  [body(): near = lax.ppermute(jnp.concatenate([hid_other, hid_own]), 'section', NEAR)]
    ppermute x1, waiting for transfers between devices: 6.92 us -> 4.92 us  [body(): far_other = lax.ppermute(hid_other, 'section', FAR)]
    ppermute x1, waiting for transfers between devices: 0.32 us -> 2.09 us  [body(): far_own = lax.ppermute(hid_own, 'section', FAR)]
    pallas_call x0 -> x1, Pallas kernels: none -> 1.63 us  [join(): pl.pallas_call(join_kernel, out_shape=jax.ShapeDtypeStruct((mine.shape[0]...]
where the time goes in v6:
time: 144 us; the launch traced here: 143 us
  waiting for transfers between devices  68.4 us (48%)
  starting transfers between devices  64.1 us (45%)
  Pallas kernels  4.89 us (3%)
  matrix products  2.64 us (2%)
  local copies, waits for them, and re-layouts  2.49 us (2%)
    all_to_all x1, waiting for transfers between devices, body(): lax.all_to_all(rows, ('section', 'expert', 'dp'), split_axis=0, concat_ax...  29.9 us
    all_to_all x1, starting transfers between devices, body(): lax.all_to_all(rows, ('section', 'expert', 'dp'), split_axis=0, concat_ax...  28.8 us
    all_to_all x1, waiting for transfers between devices, body(): lax.all_to_all(back_rows, ('expert', 'dp'), split_axis=0, concat_axis=0,...  23.8 us
    all_to_all x1, starting transfers between devices, body(): lax.all_to_all(back_rows, ('expert', 'dp'), split_axis=0, concat_axis=0,...  10.5 us
    ppermute x1, starting transfers between devices, body(): far_own = lax.ppermute(hid_own, 'section', FAR)  6.23 us
    ppermute x1, waiting for transfers between devices, body(): far_other = lax.ppermute(hid_other, 'section', FAR)  4.92 us
    ppermute x1, waiting for transfers between devices, body(): near = lax.ppermute(jnp.concatenate([hid_other, hid_own]), 'section', NEAR)  4.61 us
    ppermute x1, starting transfers between devices, body(): diagonal_other = lax.ppermute(hid_other, 'section', DIAGONAL)  4.21 us
  transfers between devices with their start and end apart: 9, of which 7 were waited for; matrix products, arithmetic and copies ran while one was open for 2% of the time, Pallas kernels for 2%

profile of v6, /device:TPU:1, one launch (start us, length us, event | category | flops | bytes accessed | tf_op | source)
XLA Modules:
  0.0 143.1 jit_solution(15421204283744974216)
XLA Ops:
  0.0 4.1 %collective-permute-start.1 = (bf16[352,2048]{1,0:T(8,128)(2,1)}, bf16[352,2048]{1,0:T(8,128)(2,1)S(1)}, u32[]{:S(2)}, u32[]{:S(2)}) collective-permute-start(bf16[352,2048]{1,0:T(8,128)(2,1)} %bitcast.42), channel_id=1, source_target_pairs={{0,256},{256,0},{512,768},{768,512},{1,257},{257,1},{513,769},{769... | collective-permute-start | bytes 4325384 | tf_op jit(solution)/shard_map/ppermute | solution.py:162
  4.2 2.8 %gated_rows.1 = bf16[256,2,1024]{2,1,0:T(2,128)(2,1)} custom-call(s32[1]{0:T(128)} %bitcast.8.kind_ref, f32[64]{0:T(128)} %table_ref.1, s32[2,128]{1,0:T(2,128)} %bitcast.39, s32[2,128]{1,0:T(2,128)} %bitcast.41, bf16[128,2048]{1,0:T(8,128)(2,1)} %up_ref.1), custom_call_target="tpu_custom_call" | custom-call | tf_op jit(solution)/shard_map/gated_rows/pallas_call | solution.py:69
  7.0 28.8 %all-to-all-start = ((bf16[256,2,1024]{2,1,0:T(2,128)(2,1)}), bf16[256,2,1024]{2,1,0:T(2,128)(2,1)S(1)}, u32[]{:S(2)}, u32[]{:S(2)}) async-start(bf16[256,2,1024]{2,1,0:T(2,128)(2,1)} %gated_rows.1), calls=%async_computation | async-start | bytes 2097152 | tf_op jit(solution)/shard_map/all_to_all | solution.py:152
  35.8 3.3 %collective-permute-start = (bf16[352,256]{1,0:T(8,128)(2,1)S(1)}, bf16[352,256]{1,0:T(8,128)(2,1)S(1)}, u32[]{:S(2)}, u32[]{:S(2)}) collective-permute-start(bf16[352,256]{1,0:T(8,128)(2,1)S(1)} %select_bitcast_fusion), channel_id=1, source_target_pairs={{0,256},{256,0},{512,768},{768,512},{1,257},{257,1},{513,769},{769... | collective-permute-start | bytes 540680 | tf_op jit(solution)/shard_map/ppermute | solution.py:165
  39.2 29.9 %all-to-all-done = bf16[256,2,1024]{2,1,0:T(2,128)(2,1)S(1)} async-done(((bf16[256,2,1024]{2,1,0:T(2,128)(2,1)}), bf16[256,2,1024]{2,1,0:T(2,128)(2,1)S(1)}, u32[]{:S(2)}, u32[]{:S(2)}) %all-to-all-start) | async-done | bytes 1048608 | tf_op jit(solution)/shard_map/all_to_all | solution.py:152
  69.4 1.1 copy-done.3
  70.5 0.6 fusion.1.after_ref
  71.0 6.2 %collective-permute-start.2 = (bf16[352,256]{1,0:T(8,128)(2,1)S(1)}, bf16[352,256]{1,0:T(8,128)(2,1)S(1)}, u32[]{:S(2)}, u32[]{:S(2)}) collective-permute-start(bf16[352,256]{1,0:T(8,128)(2,1)S(1)} %fusion.1.after_ref), channel_id=1, source_target_pairs={{0,512},{512,0},{256,768},{768,256},{1,513},{513,1},{257,769},{769... | collective-permute-start | bytes 540680 | tf_op jit(solution)/shard_map/ppermute | solution.py:174
  77.3 0.6 fusion.2
  77.9 1.9 %collective-permute-start.3 = (bf16[352,256]{1,0:T(8,128)(2,1)S(1)}, bf16[352,256]{1,0:T(8,128)(2,1)S(1)}, u32[]{:S(2)}, u32[]{:S(2)}) collective-permute-start(bf16[352,256]{1,0:T(8,128)(2,1)S(1)} %fusion.2), channel_id=1, source_target_pairs={{0,512},{512,0},{256,768},{768,256},{1,513},{513,1},{257,769},{769... | collective-permute-start | bytes 540680 | tf_op jit(solution)/shard_map/ppermute | solution.py:178
  79.8 3.1 %collective-permute-start.4 = (bf16[704,256]{1,0:T(8,128)(2,1)S(1)}, bf16[704,256]{1,0:T(8,128)(2,1)S(1)}, u32[]{:S(2)}, u32[]{:S(2)}) collective-permute-start(bf16[704,256]{1,0:T(8,128)(2,1)S(1)} %pad_maximum_fusion), channel_id=1, source_target_pairs={{0,256},{256,0},{512,768},{768,512},{1,257},{257,1},{513,769},{769... | collective-permute-start | bytes 1081352 | tf_op jit(solution)/shard_map/ppermute | solution.py:177
  83.0 4.2 %collective-permute-start.5 = (bf16[352,256]{1,0:T(8,128)(2,1)S(1)}, bf16[352,256]{1,0:T(8,128)(2,1)S(1)}, u32[]{:S(2)}, u32[]{:S(2)}) collective-permute-start(bf16[352,256]{1,0:T(8,128)(2,1)S(1)} %fusion.2), channel_id=1, source_target_pairs={{0,768},{768,0},{256,512},{512,256},{1,769},{769,1},{257,513},{513... | collective-permute-start | bytes 540680 | tf_op jit(solution)/shard_map/ppermute | solution.py:179
  87.7 2.1 %collective-permute-done.2 = bf16[352,256]{1,0:T(8,128)(2,1)S(1)} collective-permute-done((bf16[352,256]{1,0:T(8,128)(2,1)S(1)}, bf16[352,256]{1,0:T(8,128)(2,1)S(1)}, u32[]{:S(2)}, u32[]{:S(2)}) %collective-permute-start.2) | collective-permute-done | bytes 180256 | tf_op jit(solution)/shard_map/ppermute | solution.py:174
  89.8 1.9 %collective-permute-start.6 = (bf16[352,256]{1,0:T(8,128)(2,1)S(1)}, bf16[352,256]{1,0:T(8,128)(2,1)S(1)}, u32[]{:S(2)}, u32[]{:S(2)}) collective-permute-start(bf16[352,256]{1,0:T(8,128)(2,1)S(1)} %collective-permute-done.2), channel_id=1, source_target_pairs={{0,256},{256,0},{512,768},{768,512},{1,257},{257,1},{513,769},{769... | collective-permute-start | bytes 540680 | tf_op jit(solution)/shard_map/ppermute | solution.py:180
  91.7 4.9 %collective-permute-done.3 = bf16[352,256]{1,0:T(8,128)(2,1)S(1)} collective-permute-done((bf16[352,256]{1,0:T(8,128)(2,1)S(1)}, bf16[352,256]{1,0:T(8,128)(2,1)S(1)}, u32[]{:S(2)}, u32[]{:S(2)}) %collective-permute-start.3) | collective-permute-done | bytes 180256 | tf_op jit(solution)/shard_map/ppermute | solution.py:178
  96.6 0.6 convolution_convert_fusion.mine_ref
  97.2 0.6 collective-permute-done.5.diagonal_ref
  97.8 4.6 %collective-permute-done.4.near_ref = bf16[704,256]{1,0:T(8,128)(2,1)S(1)} collective-permute-done((bf16[704,256]{1,0:T(8,128)(2,1)S(1)}, bf16[704,256]{1,0:T(8,128)(2,1)S(1)}, u32[]{:S(2)}, u32[]{:S(2)}) %collective-permute-start.4) | collective-permute-done | bytes 360480 | tf_op jit(solution)/shard_map/ppermute | solution.py:177
  102.5 2.3 %collective-permute-done.6.relay_ref = bf16[352,256]{1,0:T(8,128)(2,1)S(1)} collective-permute-done((bf16[352,256]{1,0:T(8,128)(2,1)S(1)}, bf16[352,256]{1,0:T(8,128)(2,1)S(1)}, u32[]{:S(2)}, u32[]{:S(2)}) %collective-permute-start.6) | collective-permute-done | bytes 180256 | tf_op jit(solution)/shard_map/ppermute | solution.py:180
  104.8 1.6 %join.1 = bf16[256,2,512]{2,1,0:T(2,128)(2,1)} custom-call(bf16[256,512]{1,0:T(8,128)(2,1)S(1)} %convolution_convert_fusion.mine_ref, bf16[704,256]{1,0:T(8,128)(2,1)S(1)} %collective-permute-done.4.near_ref, bf16[352,256]{1,0:T(8,128)(2,1)S(1)} %collective-permute-done.5.diagonal_ref, bf16[352,256]{1,0:T(8,128)(2,1)S(1)} %collective-permute-done.6.relay_ref, ...), custom_call_target="tpu_custom_call" | custom-call | tf_op jit(solution)/shard_map/join/pallas_call | solution.py:96
  106.4 10.5 %all-to-all-start.1 = ((bf16[256,2,512]{2,1,0:T(2,128)(2,1)}), bf16[256,2,512]{2,1,0:T(2,128)(2,1)S(1)}, u32[]{:S(2)}, u32[]{:S(2)}) async-start(bf16[256,2,512]{2,1,0:T(2,128)(2,1)} %join.1), calls=%async_computation.1 | async-start | bytes 1048576 | tf_op jit(solution)/shard_map/all_to_all | solution.py:192
  116.9 0.9 constant_dynamic-slice_fusion
  118.2 23.8 %all-to-all-done.1 = bf16[256,2,512]{2,1,0:T(2,128)(2,1)S(1)} async-done(((bf16[256,2,512]{2,1,0:T(2,128)(2,1)}), bf16[256,2,512]{2,1,0:T(2,128)(2,1)S(1)}, u32[]{:S(2)}, u32[]{:S(2)}) %all-to-all-start.1) | async-done | bytes 524320 | tf_op jit(solution)/shard_map/all_to_all | solution.py:192
  142.3 0.9 fusion.3
  (20 shorter events, 1.3 us)
Async XLA Ops:
  0.0 39.2 %collective-permute-start.1 = (bf16[352,2048]{1,0:T(8,128)(2,1)}, bf16[352,2048]{1,0:T(8,128)(2,1)S(1)}, u32[]{:S(2)}, u32[]{:S(2)}) collective-permute-start(bf16[352,2048]{1,0:T(8,128)(2,1)} %bitcast.42), channel_id=1, source_target_pairs={{0,256},{256,0},{512,768},{768,512},{1,257},{257,1},{513,769},{769... | collective-permute-start | bytes 4325384 | tf_op jit(solution)/shard_map/ppermute | solution.py:162
  7.0 28.8 %copy-start.1 = (bf16[1,256,2,352]{1,3,2,0:T(8,128)(2,1)S(1)}, bf16[1,256,2,352]{1,3,2,0:T(8,128)(2,1)}, u32[]{:S(2)}) copy-start(bf16[1,256,2,352]{1,3,2,0:T(8,128)(2,1)} %param.13) | copy-start | bytes 1081348
  7.0 62.1 %all-to-all-start = ((bf16[256,2,1024]{2,1,0:T(2,128)(2,1)}), bf16[256,2,1024]{2,1,0:T(2,128)(2,1)S(1)}, u32[]{:S(2)}, u32[]{:S(2)}) async-start(bf16[256,2,1024]{2,1,0:T(2,128)(2,1)} %gated_rows.1), calls=%async_computation | async-start | bytes 2097152 | tf_op jit(solution)/shard_map/all_to_all | solution.py:152
  35.8 41.4 %collective-permute-start = (bf16[352,256]{1,0:T(8,128)(2,1)S(1)}, bf16[352,256]{1,0:T(8,128)(2,1)S(1)}, u32[]{:S(2)}, u32[]{:S(2)}) collective-permute-start(bf16[352,256]{1,0:T(8,128)(2,1)S(1)} %select_bitcast_fusion), channel_id=1, source_target_pairs={{0,256},{256,0},{512,768},{768,512},{1,257},{257,1},{513,769},{769... | collective-permute-start | bytes 540680 | tf_op jit(solution)/shard_map/ppermute | solution.py:165
  69.1 1.4 copy-start.3
  71.0 18.7 %collective-permute-start.2 = (bf16[352,256]{1,0:T(8,128)(2,1)S(1)}, bf16[352,256]{1,0:T(8,128)(2,1)S(1)}, u32[]{:S(2)}, u32[]{:S(2)}) collective-permute-start(bf16[352,256]{1,0:T(8,128)(2,1)S(1)} %fusion.1.after_ref), channel_id=1, source_target_pairs={{0,512},{512,0},{256,768},{768,256},{1,513},{513,1},{257,769},{769... | collective-permute-start | bytes 540680 | tf_op jit(solution)/shard_map/ppermute | solution.py:174
  77.3 9.9 %copy-start = (bf16[1,512,1408]{2,1,0:T(8,128)(2,1)S(1)}, bf16[1,512,1408]{2,1,0:T(8,128)(2,1)}, u32[]{:S(2)}) copy-start(bf16[1,512,1408]{2,1,0:T(8,128)(2,1)} %param.11) | copy-start | bytes 4325380
  77.9 18.7 %collective-permute-start.3 = (bf16[352,256]{1,0:T(8,128)(2,1)S(1)}, bf16[352,256]{1,0:T(8,128)(2,1)S(1)}, u32[]{:S(2)}, u32[]{:S(2)}) collective-permute-start(bf16[352,256]{1,0:T(8,128)(2,1)S(1)} %fusion.2), channel_id=1, source_target_pairs={{0,512},{512,0},{256,768},{768,256},{1,513},{513,1},{257,769},{769... | collective-permute-start | bytes 540680 | tf_op jit(solution)/shard_map/ppermute | solution.py:178
  79.8 22.6 %collective-permute-start.4 = (bf16[704,256]{1,0:T(8,128)(2,1)S(1)}, bf16[704,256]{1,0:T(8,128)(2,1)S(1)}, u32[]{:S(2)}, u32[]{:S(2)}) collective-permute-start(bf16[704,256]{1,0:T(8,128)(2,1)S(1)} %pad_maximum_fusion), channel_id=1, source_target_pairs={{0,256},{256,0},{512,768},{768,512},{1,257},{257,1},{513,769},{769... | collective-permute-start | bytes 1081352 | tf_op jit(solution)/shard_map/ppermute | solution.py:177
  83.0 14.9 %collective-permute-start.5 = (bf16[352,256]{1,0:T(8,128)(2,1)S(1)}, bf16[352,256]{1,0:T(8,128)(2,1)S(1)}, u32[]{:S(2)}, u32[]{:S(2)}) collective-permute-start(bf16[352,256]{1,0:T(8,128)(2,1)S(1)} %fusion.2), channel_id=1, source_target_pairs={{0,768},{768,0},{256,512},{512,256},{1,769},{769,1},{257,513},{513... | collective-permute-start | bytes 540680 | tf_op jit(solution)/shard_map/ppermute | solution.py:179
  89.8 15.0 %collective-permute-start.6 = (bf16[352,256]{1,0:T(8,128)(2,1)S(1)}, bf16[352,256]{1,0:T(8,128)(2,1)S(1)}, u32[]{:S(2)}, u32[]{:S(2)}) collective-permute-start(bf16[352,256]{1,0:T(8,128)(2,1)S(1)} %collective-permute-done.2), channel_id=1, source_target_pairs={{0,256},{256,0},{512,768},{768,512},{1,257},{257,1},{513,769},{769... | collective-permute-start | bytes 540680 | tf_op jit(solution)/shard_map/ppermute | solution.py:180
  97.2 20.6 %copy-start.2 = (s32[128,2]{0,1:T(2,128)S(1)}, s32[128,2]{0,1:T(2,128)}, u32[]{:S(2)}) copy-start(s32[128,2]{0,1:T(2,128)} %param.8) | copy-start | bytes 3076
  106.4 35.6 %all-to-all-start.1 = ((bf16[256,2,512]{2,1,0:T(2,128)(2,1)}), bf16[256,2,512]{2,1,0:T(2,128)(2,1)S(1)}, u32[]{:S(2)}, u32[]{:S(2)}) async-start(bf16[256,2,512]{2,1,0:T(2,128)(2,1)} %join.1), calls=%async_computation.1 | async-start | bytes 1048576 | tf_op jit(solution)/shard_map/all_to_all | solution.py:192
